TPU v7x, 128 devices: a whole 4x4x4 slice. The times are simulated.
128 devices in a mesh: dp: 4 (over y_lo, core), cent: 32 (over x, y_hi, z).
Axes of the slice: x: 4, y: 4 (y_hi: 2, y_lo: 2; y = y_hi * 2 + y_lo), z: 4, core: 2. Of those that a mesh axis runs over, the one named last changes fastest.
Arguments:
- queries: bfloat16 [2048, 768], P('dp')
- centroids: bfloat16 [16384, 768], P('cent'), as said below
- beta: float32 [2048], P('dp'), may hold values from 16 to 400
- teacher_ids: int32 [2048, 16], P('dp'), may hold values from 0 to 16383
Outputs:
- query_grad: float32 [2048, 768], P(('dp', 'cent'))
- centroid_grad: float32 [16384, 768], P('cent', 'dp')
Inputs may be any that keep to these rules, and one draw needn't show every extreme that they name: `centroids`: each centroid row has length one before rounding to bfloat16.
All inputs are finite; a program needn't handle non-finite values.
Results may differ from a plain program's by a relative error of at most 0.0098.
Values may be sent and summed in bfloat16 or wider, within the bound.
A program may use at most 64 MiB of HBM per device.

v0:
```python
import jax
import jax.numpy as jnp
from jax import lax
from jax.sharding import PartitionSpec as P

grad_scale = 1024.0
eps = 1e-06


def local(queries, centroids, beta, teacher_ids):
    query_rows = queries.shape[0]
    cent_rows = centroids.shape[0]
    topk_count = teacher_ids.shape[1]
    query_float = queries.astype(jnp.float32)
    qnorm = jnp.sqrt(jnp.sum(query_float * query_float, axis=1) + eps)
    qhat = (query_float / qnorm[:, None]).astype(jnp.bfloat16)
    cosine = jnp.einsum("bd,kd->bk", qhat, centroids, preferred_element_type=jnp.float32)
    score = beta[:, None] * cosine
    local_top = jnp.max(score, axis=1)
    row_top = lax.pmax(local_top, "cent")
    expo = jnp.exp(score - row_top[:, None])
    total = lax.psum(jnp.sum(expo, axis=1), "cent")
    prob = expo / total[:, None]
    offset = lax.axis_index("cent") * cent_rows
    local_ids = teacher_ids - offset
    column_pos = jnp.arange(cent_rows, dtype=jnp.int32)[None, :]
    counts = jnp.zeros((query_rows, cent_rows), jnp.float32)
    for slot in range(topk_count):
        counts = counts + (local_ids[:, slot : slot + 1] == column_pos).astype(jnp.float32)
    target = counts * (1.0 / topk_count)
    dscore = (grad_scale * (prob - target)).astype(jnp.bfloat16)
    share_rows = query_rows // lax.axis_size("cent")
    qshare = lax.psum_scatter(
        jnp.dot(dscore, centroids, preferred_element_type=jnp.float32),
        "cent",
        scatter_dimension=0,
        tiled=True,
    )
    first_row = lax.axis_index("cent") * share_rows
    own_hat = lax.dynamic_slice_in_dim(qhat, first_row, share_rows, 0).astype(jnp.float32)
    own_norm = lax.dynamic_slice_in_dim(qnorm, first_row, share_rows, 0)
    along = jnp.sum(qshare * own_hat, axis=1)
    query_grad = (qshare - along[:, None] * own_hat) / own_norm[:, None]
    width = queries.shape[1]
    col_count = width // lax.axis_size("dp")
    first_col = lax.axis_index("dp") * col_count
    partial_grad = jnp.einsum("bk,bd->kd", dscore, qhat, preferred_element_type=jnp.float32)
    cgrad = lax.psum_scatter(partial_grad, "dp", scatter_dimension=1, tiled=True)
    cent_cols = lax.dynamic_slice_in_dim(centroids, first_col, col_count, 1).astype(jnp.float32)
    rowdot = lax.psum(jnp.sum(cent_cols * cgrad, axis=1), "dp")
    centroid_grad = cgrad - rowdot[:, None] * cent_cols
    return (query_grad, centroid_grad)


def solution(mesh):
    in_specs = (P("dp", None), P("cent", None), P("dp"), P("dp", None))
    out_specs = (P(("dp", "cent"), None), P("cent", "dp"))
    return jax.shard_map(local, mesh=mesh, in_specs=in_specs, out_specs=out_specs, check_vma=False)
```

profile of v0, /device:TPU:1, one launch (start us, length us, event | category | flops | bytes accessed | tf_op | source)
XLA Modules:
  0.0 460.0 jit_solution(17168080293541555458)
XLA Ops:
  7.2 0.0 copy-start
  7.2 0.0 reduce-scatter.5.cloned.1.call-start
  7.2 1.4 fusion
  8.7 1.4 fusion.1
  10.1 0.6 fusion.9
  10.8 84.7 %pmax.7 = f32[512]{0:T(512)S(1)} all-reduce(f32[512]{0:T(512)S(1)} %get-tuple-element.18), channel_id=1, replica_groups=mesh['dp'=4,'cent'=32] {'cent'}, use_global_device_ids=true, to_apply=%region_2.0 | all-reduce | flops 512 | bytes 4096 | tf_op jit(solution)/shard_map/pmax | solution.py:20
  95.4 0.2 fusion.2
  95.6 75.3 %psum.14 = f32[512]{0:T(512)S(1)} all-reduce(f32[512]{0:T(512)S(1)} %fusion.2), channel_id=1, replica_groups=mesh['dp'=4,'cent'=32] {'cent'}, use_global_device_ids=true, to_apply=%region_4.0 | all-reduce | flops 512 | bytes 4096 | tf_op jit(solution)/shard_map/psum | solution.py:22
  170.9 2.3 multiply_convert_fusion
  173.2 1.8 fusion.11
  174.9 0.0 reduce-scatter.5.cloned.1.call-update
  175.0 0.0 reduce-scatter.3.cloned.1.call-start
  175.0 1.7 fusion.10
  176.7 0.0 reduce-scatter.3.cloned.1.call-update
  176.8 0.1 dynamic_slice.10
  176.9 0.1 constant_dynamic-slice_fusion
  177.0 0.1 copy.7
  177.1 45.0 %reduce-scatter.5.cloned.1.call-done = f32[512,192]{0,1:T(8,128)} async-done(((f32[512,768]{0,1:T(8,128)}), f32[512,192]{0,1:T(8,128)}) %reduce-scatter.5.cloned.1.call-update) | async-done | bytes 393232 | tf_op jit(solution)/shard_map/reduce_scatter | solution.py:48
  222.2 1.1 fusion.3
  223.2 5.4 %psum.15 = f32[512]{0:T(512)S(1)} all-reduce(f32[512]{0:T(512)S(1)} %fusion.3), channel_id=1, replica_groups=mesh['dp'=4,'cent'=32] {'dp'}, use_global_device_ids=true, to_apply=%region_9.0 | all-reduce | flops 512 | bytes 4096 | tf_op jit(solution)/shard_map/psum | solution.py:50
  228.7 220.3 %reduce-scatter.3.cloned.1.call-done = f32[16,768]{1,0:T(8,128)} async-done(((f32[512,768]{1,0:T(8,128)}), f32[16,768]{1,0:T(8,128)}) %reduce-scatter.3.cloned.1.call-update) | async-done | bytes 49168 | tf_op jit(solution)/shard_map/reduce_scatter | solution.py:33
  448.9 0.9 fusion.5
  449.9 1.8 fusion.4
  451.7 1.5 fusion.7
  (8 shorter events, 0.1 us)
Async XLA Ops:
  7.2 3.0 copy-start
  7.2 2.9 copy-start.1
  7.2 2.9 copy-start.2
  7.2 215.0 %reduce-scatter.5.cloned.1.call-start = ((), (), s32[]{:S(2)}) async-start(), calls=%async_computation.3 | async-start | bytes 1966080 | tf_op jit(solution)/shard_map/reduce_scatter | solution.py:48
  175.0 274.0 %reduce-scatter.3.cloned.1.call-start = ((), (), s32[]{:S(2)}) async-start(), calls=%async_computation.2 | async-start | bytes 1622016 | tf_op jit(solution)/shard_map/reduce_scatter | solution.py:33
Sparse Core Ops, SparseCore 0:
  175.1 47.0 reduce-scatter.4
  227.1 221.7 reduce-scatter.2
where the time goes:
time: 462 us; the launch traced here: 460 us
  waiting for transfers between devices  265 us (57%)
  blocking collectives  165 us (36%)
  between operations  14.1 us (3%)
  other arithmetic  10.5 us (2%)
    reduce_scatter x1, waiting for transfers between devices, local(): lax.psum_scatter(jnp.dot(dscore, centroids, preferred_element_type=jnp.fl...  220 us
    pmax x1, blocking collectives, local(): row_top = lax.pmax(local_top, 'cent')  84.7 us
    psum x1, blocking collectives, local(): total = lax.psum(jnp.sum(expo, axis=1), 'cent')  75.3 us
    reduce_scatter x1, waiting for transfers between devices, local(): lax.psum_scatter(partial_grad, 'dp', scatter_dimension=1, tiled=True)  45 us
  transfers between devices with their start and end apart: 2, of which 2 were waited for; matrix products, arithmetic and copies ran while one was open for 1% of the time, Pallas kernels for 0%

commit v1 on v0

v1 whole, which is shorter than its diff:
```python
import functools

import jax
import jax.numpy as jnp
from jax import lax
from jax.experimental import pallas as pl
from jax.experimental.pallas import tpu as pltpu
from jax.sharding import PartitionSpec as P

EPS = 1e-06
SCALE = 1024.0
MESH = pl.DeviceIdType.MESH
F32 = jnp.float32
BF16 = jnp.bfloat16
NT = (((1,), (1,)), ((), ()))
TN = (((0,), (0,)), ((), ()))


def dot(a, b, dims):
    return lax.dot_general(a, b, dims, preferred_element_type=F32)


def kernel(
    q_hbm, c_hbm, beta_hbm, ids_hbm,
    qg_ref, cg_ref,
    q_v, c_v, beta_v, ids_v,
    qh_v, qht_v, ct_v, cos_v, e_v, d_v,
    es_v, ts_v,
    lse_s, lse_r,
    gx_s, gx_r, gz_s, gz_r,
    bx_s, bx_r, bz_s, bz_r,
    core_s, core_r, y_s, y_r,
    row_s, row_r,
    in_sem, lse_sem, a_send, a_recv, b_sem, core_send, core_recv, y_sem, row_sem,
):
    rows, width = q_hbm.shape
    cells = c_hbm.shape[0]
    slots = ids_hbm.shape[0]
    half = width // 2
    part = width // 4
    dp = lax.axis_index("dp")
    cent = lax.axis_index("cent")
    x = cent // 8
    yhi = (cent // 4) % 2
    z = cent % 4
    core = dp % 2
    ylo = dp // 2

    loads = [
        pltpu.make_async_copy(src, dst, in_sem.at[i])
        for i, (src, dst) in enumerate(((q_hbm, q_v), (c_hbm, c_v), (beta_hbm, beta_v), (ids_hbm, ids_v)))
    ]
    for load in loads:
        load.start()

    barrier = pltpu.get_barrier_semaphore()

    @pl.loop(1, 32)
    def _(r):
        pl.semaphore_signal(barrier, inc=1, device_id=(dp, (cent + r) % 32), device_id_type=MESH)

    @pl.loop(1, 4)
    def _(r):
        pl.semaphore_signal(barrier, inc=1, device_id=((dp + r) % 4, cent), device_id_type=MESH)

    loads[0].wait()
    for i in range(4):
        block = pl.ds(i * (rows // 4), rows // 4)
        qf = q_v[block, :].astype(F32)
        inv = 1.0 / jnp.sqrt(jnp.sum(qf * qf, axis=1, keepdims=True) + EPS)
        qh_v[block, :] = (qf * inv).astype(BF16)

    loads[1].wait()
    loads[2].wait()
    loads[3].wait()
    tops = []
    for i in range(2):
        lanes = pl.ds(i * (rows // 2), rows // 2)
        cosine = dot(c_v[...], qh_v[lanes, :], NT)
        cos_v[:, lanes] = cosine
        score = cosine * beta_v[:, lanes]
        top = jnp.max(score, axis=0, keepdims=True)
        expo = jnp.exp(score - top)
        e_v[:, lanes] = expo
        lse_s[0, :, lanes] = top + jnp.log(jnp.sum(expo, axis=0, keepdims=True))
        tops.append(top)

    pl.semaphore_wait(barrier, 34)

    def lse_copy(r):
        return pltpu.make_async_remote_copy(
            src_ref=lse_s.at[0],
            dst_ref=lse_r.at[r - 1],
            send_sem=lse_sem.at[0],
            recv_sem=lse_sem.at[1],
            device_id=(dp, (cent + r) % 32),
            device_id_type=MESH,
        )

    @pl.loop(1, 32)
    def _(r):
        lse_copy(r).start()

    qht_v[...] = qh_v[...].T
    ct_v[...] = c_v[...].T
    first = cent * cells
    for i in range(2):
        lanes = pl.ds(i * (rows // 2), rows // 2)
        cell_pos = lax.broadcasted_iota(jnp.int32, (cells, rows // 2), 0) + first
        count = jnp.zeros((cells, rows // 2), F32)
        for slot in range(slots):
            count = count + jnp.where(ids_v[slot : slot + 1, lanes] == cell_pos, SCALE / slots, 0.0)
        d_v[:, lanes] = count
        e = e_v[:, lanes]
        high = e.astype(BF16)
        low = (e - high.astype(F32)).astype(BF16)
        es_v[lanes, :] = dot(high, c_v[...], TN) + dot(low, c_v[...], TN)
        ts_v[lanes, :] = dot(count.astype(BF16), c_v[...], TN)

    pltpu.make_async_copy(lse_r, lse_r, lse_sem.at[1]).wait()
    own = lse_s[0]
    others = lse_r[...]
    top_all = jnp.maximum(jnp.max(others, axis=0), own)
    lse = top_all + jnp.log(jnp.sum(jnp.exp(others - top_all[None]), axis=0) + jnp.exp(own - top_all))
    weight = jnp.exp(jnp.concatenate(tops, axis=1) - lse) * SCALE
    weight_col = jnp.broadcast_to(weight, (128, rows)).T

    for i in range(rows // 128):
        block = pl.ds(i * 128, 128)
        for j in range(3):
            cols = pl.ds(j * 128, 128)
            gx_s[i, :, cols] = (es_v[block, cols] * weight_col[i * 128 : (i + 1) * 128] - ts_v[block, cols]).astype(BF16)
        for j in range(3):
            cols = pl.ds(half + j * 128, 128)
            g = (es_v[block, cols] * weight_col[i * 128 : (i + 1) * 128] - ts_v[block, cols]).astype(BF16)
            for k in range(8):
                gz_s[k % 4, 2 * i + k // 4, :, pl.ds(j * 128, 128)] = g[k * 16 : (k + 1) * 16]

    def x_copy(r):
        to = (x + r) % 4
        return pltpu.make_async_remote_copy(
            src_ref=gx_s.at[to], dst_ref=gx_r.at[r - 1], send_sem=a_send.at[0, r - 1], recv_sem=a_recv.at[0, r - 1],
            device_id=(dp, (to * 2 + yhi) * 4 + z), device_id_type=MESH,
        )

    def z_copy(r):
        to = (z + r) % 4
        return pltpu.make_async_remote_copy(
            src_ref=gz_s.at[to], dst_ref=gz_r.at[r - 1], send_sem=a_send.at[1, r - 1], recv_sem=a_recv.at[1, r - 1],
            device_id=(dp, (x * 2 + yhi) * 4 + to), device_id_type=MESH,
        )

    for r in (2, 1, 3):
        x_copy(r).start()
        z_copy(r).start()

    d = (e_v[...] * weight - d_v[...]).astype(BF16)
    df = d.astype(F32)

    def grad_part(to):
        return dot(qht_v[pl.ds(pl.multiple_of(to * part, 64), part), :], d, NT)

    def core_copy(i):
        return pltpu.make_async_remote_copy(
            src_ref=core_s.at[i], dst_ref=core_r.at[i], send_sem=core_send.at[i], recv_sem=core_recv.at[i],
            device_id=(ylo * 2 + 1 - core, cent), device_id_type=MESH,
        )

    y_copy = pltpu.make_async_remote_copy(
        src_ref=y_s, dst_ref=y_r, send_sem=y_sem.at[0], recv_sem=y_sem.at[1],
        device_id=((1 - ylo) * 2 + core, cent), device_id_type=MESH,
    )

    core_s[0] = grad_part((1 - ylo) * 2 + 1 - core).astype(BF16)
    core_copy(0).start()
    core_s[1] = grad_part(ylo * 2 + 1 - core).astype(BF16)
    core_copy(1).start()
    far = grad_part((1 - ylo) * 2 + core)
    core_copy(0).wait()
    y_s[...] = (far + core_r[0].astype(F32)).astype(BF16)
    y_copy.start()
    near = grad_part(dp)

    prod = df * cos_v[...]
    prod = prod[:, 0:128] + prod[:, 128:256] + prod[:, 256:384] + prod[:, 384:512]
    rowdot = jnp.sum(prod.T, axis=0, keepdims=True)
    row_s[...] = rowdot

    def row_copy(r):
        return pltpu.make_async_remote_copy(
            src_ref=row_s, dst_ref=row_r.at[r - 1], send_sem=row_sem.at[0, r - 1], recv_sem=row_sem.at[1, r - 1],
            device_id=((dp + r) % 4, cent), device_id_type=MESH,
        )

    for r in range(1, 4):
        row_copy(r).start()
    core_copy(1).wait()
    near = near + core_r[1].astype(F32)

    def bx_copy(r):
        tz = (z + r) % 4
        ty = (yhi + r // 4) % 2
        return pltpu.make_async_remote_copy(
            src_ref=bx_s.at[ty * 4 + tz], dst_ref=bx_r.at[r - 1], send_sem=b_sem.at[0], recv_sem=b_sem.at[1],
            device_id=(dp, (x * 2 + ty) * 4 + tz), device_id_type=MESH,
        )

    def bz_copy(r):
        tx = (x + r) % 4
        ty = (yhi + r // 4) % 2
        return pltpu.make_async_remote_copy(
            src_ref=bz_s.at[tx * 2 + ty], dst_ref=bz_r.at[r - 1], send_sem=b_sem.at[2], recv_sem=b_sem.at[3],
            device_id=(dp, (tx * 2 + ty) * 4 + z), device_id_type=MESH,
        )

    for r in range(1, 4):
        x_copy(r).wait()
    total = gx_s[x].astype(F32)
    for r in range(3):
        total = total + gx_r[r].astype(F32)
    bx_s[...] = total.astype(BF16).reshape(8, 16, half)

    @pl.loop(1, 8)
    def _(r):
        bx_copy(r).start()

    for r in range(1, 4):
        z_copy(r).wait()
    total = gz_s[z].astype(F32)
    for r in range(3):
        total = total + gz_r[r].astype(F32)
    bz_s[...] = total.astype(BF16)

    @pl.loop(1, 8)
    def _(r):
        bz_copy(r).start()

    y_copy.wait()
    for r in range(1, 4):
        row_copy(r).wait()
        rowdot = rowdot + row_r[r - 1]
    near = near + y_r[...].astype(F32)
    own_cent = ct_v[pl.ds(pl.multiple_of(dp * part, 64), part), :].astype(F32)
    cg_ref[...] = (near - rowdot * own_cent).T

    mine = pl.ds(pl.multiple_of(cent * 16, 16), 16)
    qf = q_v[mine, :].astype(F32)
    norm = jnp.sqrt(jnp.sum(qf * qf, axis=1, keepdims=True) + EPS)
    hat = qh_v[mine, :].astype(F32)
    pltpu.make_async_copy(bx_r, bx_r, b_sem.at[1]).wait()
    left = bx_s[yhi * 4 + z].astype(F32) + jnp.sum(bx_r[...].astype(F32), axis=0)
    pltpu.make_async_copy(bz_r, bz_r, b_sem.at[3]).wait()
    right = bz_s[x * 2 + yhi].astype(F32) + jnp.sum(bz_r[...].astype(F32), axis=0)
    grad = jnp.concatenate([left, right], axis=1)
    along = jnp.sum(grad * hat, axis=1, keepdims=True)
    qg_ref[...] = (grad - along * hat) / norm

    pltpu.make_async_copy(lse_r, lse_r, lse_sem.at[0]).wait()
    pltpu.make_async_copy(bx_r, bx_r, b_sem.at[0]).wait()
    pltpu.make_async_copy(bz_r, bz_r, b_sem.at[2]).wait()


def local(queries, centroids, beta, teacher_ids):
    rows, width = queries.shape
    cells = centroids.shape[0]
    slots = teacher_ids.shape[1]
    half, part = width // 2, width // 4
    dma = pltpu.SemaphoreType.DMA
    return pl.pallas_call(
        kernel,
        out_shape=(
            jax.ShapeDtypeStruct((rows // 32, width), F32),
            jax.ShapeDtypeStruct((cells, part), F32),
        ),
        in_specs=[pl.BlockSpec(memory_space=pl.ANY)] * 4,
        out_specs=[pl.BlockSpec(memory_space=pltpu.VMEM)] * 2,
        scratch_shapes=[
            pltpu.VMEM((rows, width), BF16),
            pltpu.VMEM((cells, width), BF16),
            pltpu.VMEM((1, rows), F32),
            pltpu.VMEM((slots, rows), jnp.int32),
            pltpu.VMEM((rows, width), BF16),
            pltpu.VMEM((width, rows), BF16),
            pltpu.VMEM((width, cells), BF16),
            pltpu.VMEM((cells, rows), F32),
            pltpu.VMEM((cells, rows), F32),
            pltpu.VMEM((cells, rows), F32),
            pltpu.VMEM((rows, width), F32),
            pltpu.VMEM((rows, width), F32),
            pltpu.VMEM((1, 1, rows), F32),
            pltpu.VMEM((31, 1, rows), F32),
            pltpu.VMEM((4, rows // 4, half), BF16),
            pltpu.VMEM((3, rows // 4, half), BF16),
            pltpu.VMEM((4, 8, 16, half), BF16),
            pltpu.VMEM((3, 8, 16, half), BF16),
            pltpu.VMEM((8, 16, half), BF16),
            pltpu.VMEM((7, 16, half), BF16),
            pltpu.VMEM((8, 16, half), BF16),
            pltpu.VMEM((7, 16, half), BF16),
            pltpu.VMEM((2, part, cells), BF16),
            pltpu.VMEM((2, part, cells), BF16),
            pltpu.VMEM((part, cells), BF16),
            pltpu.VMEM((part, cells), BF16),
            pltpu.VMEM((1, cells), F32),
            pltpu.VMEM((3, 1, cells), F32),
            dma((4,)),
            dma((2,)),
            dma((2, 3)),
            dma((2, 3)),
            dma((4,)),
            dma((2,)),
            dma((2,)),
            dma((2,)),
            dma((2, 3)),
        ],
        compiler_params=pltpu.CompilerParams(
            collective_id=0, has_side_effects=True, vmem_limit_bytes=60 * 1024 * 1024
        ),
    )(queries, centroids, beta.reshape(1, rows), teacher_ids.T)


def solution(mesh):
    in_specs = (P("dp", None), P("cent", None), P("dp"), P("dp", None))
    out_specs = (P(("dp", "cent"), None), P("cent", "dp"))
    return jax.shard_map(local, mesh=mesh, in_specs=in_specs, out_specs=out_specs, check_vma=False)
```

time: 462 us -> 32.2 us (0.07)
  waiting for transfers between devices: 265 us -> 0 us
  blocking collectives: 165 us -> 0 us
  Pallas kernels: 0 us -> 28.7 us
  between operations: 14.1 us -> 0.65 us
  other arithmetic: 10.5 us -> 0 us
    reduce_scatter x2 -> x0, waiting for transfers between devices: 265 us -> none  [the longest x1 220 us: local(): lax.psum_scatter(jnp.dot(dscore, centroids, preferred_element_type=jnp.fl...]
    pmax x1 -> x0, blocking collectives: 84.7 us -> none  [local(): row_top = lax.pmax(local_top, 'cent')]
    psum x2 -> x0, blocking collectives: 80.7 us -> none  [the longest x1 75.3 us: local(): total = lax.psum(jnp.sum(expo, axis=1), 'cent')]
    pallas_call x0 -> x1, Pallas kernels: none -> 28.7 us  [local(): pl.pallas_call(kernel, out_shape=(jax.ShapeDtypeStruct((rows // 32, width...]
  transfers between devices with their start and end apart: 2 -> 0, of which waited for: 2 -> 0; matrix products, arithmetic and copies ran while one was open for 1% -> 0% of each run, Pallas kernels for 0% -> 0%
where the time goes in v1:
time: 32.2 us; the launch traced here: 32 us
  Pallas kernels  28.7 us (89%)
  local copies, waits for them, and re-layouts  2.61 us (8%)
  between operations  0.65 us (2%)
    pallas_call x1, Pallas kernels, local(): pl.pallas_call(kernel, out_shape=(jax.ShapeDtypeStruct((rows // 32, width...  28.7 us
    pallas_call x1, local copies, waits for them, and re-layouts, local(): pl.pallas_call(kernel, out_shape=(jax.ShapeDtypeStruct((rows // 32, width...  1.98 us

profile of v1, /device:TPU:1, one launch (start us, length us, event | category | flops | bytes accessed | tf_op | source)
XLA Modules:
  0.0 32.0 jit_solution(16885725494565453806)
XLA Ops:
  0.6 28.7 %shard_map.59 = (f32[16,768]{1,0:T(8,128)}, f32[512,192]{1,0:T(8,128)}) custom-call(bf16[512,768]{1,0:T(8,128)(2,1)} %q_hbm.1, bf16[512,768]{1,0:T(8,128)(2,1)} %c_hbm.1, f32[1,512]{1,0:T(1,128)} %bitcast.3, s32[16,512]{1,0:T(8,128)} %bitcast.2), custom_call_target="tpu_custom_call" | custom-call | tf_op jit(solution)/shard_map/pallas_call | solution.py:269
  29.4 0.0 copy-start
  29.4 2.0 %copy.6 = f32[512,192]{0,1:T(8,128)} copy(f32[512,192]{1,0:T(8,128)} %get-tuple-element.3) | data formatting | bytes 786432 | tf_op jit(solution)/shard_map/pallas_call | solution.py:269
  31.4 0.0 copy-done
  31.4 0.6 %copy.8 = f32[16,768]{1,0:T(8,128)} copy(f32[16,768]{1,0:T(8,128)S(1)} %copy-done) | data formatting | bytes 98304
Async XLA Ops:
  29.4 2.0 %copy-start = (f32[16,768]{1,0:T(8,128)S(1)}, f32[16,768]{1,0:T(8,128)}, u32[]{:S(2)}) copy-start(f32[16,768]{1,0:T(8,128)} %get-tuple-element.6) | copy-start | bytes 147460

commit v2 on v1

v2 whole, which is shorter than its diff:
```python
import functools

import jax
import jax.numpy as jnp
from jax import lax
from jax.experimental import pallas as pl
from jax.experimental.pallas import tpu as pltpu
from jax.sharding import PartitionSpec as P

EPS = 1e-06
SCALE = 1024.0
MESH = pl.DeviceIdType.MESH
F32 = jnp.float32
BF16 = jnp.bfloat16
NT = (((1,), (1,)), ((), ()))
TN = (((0,), (0,)), ((), ()))


def dot(a, b, dims):
    return lax.dot_general(a, b, dims, preferred_element_type=F32)


def join(own, others):
    top = jnp.maximum(jnp.max(others, axis=0), own)
    return top + jnp.log(jnp.sum(jnp.exp(others - top[None]), axis=0) + jnp.exp(own - top))


def kernel(
    q_hbm, c_hbm, beta_hbm, ids_hbm,
    qg_ref, cg_ref,
    q_v, c_v, beta_v, ids_v,
    qh_v, qht_v, ct_v, cos_v, e_v, d_v,
    es_v, ts_v,
    lse_s, lse_r,
    gx_s, gx_r, gz_s, gz_r,
    bx_s, bx_r, bz_s, bz_r,
    core_s, core_r, y_s, y_r,
    near_v, row_s, row_r,
    in_sem, lse_sem, a_send, a_recv, b_sem, core_send, core_recv, y_send, y_recv, row_sem, ready_sem,
):
    rows, width = q_hbm.shape
    cells = c_hbm.shape[0]
    slots = ids_hbm.shape[0]
    half = width // 2
    part = width // 4
    dp = lax.axis_index("dp")
    cent = lax.axis_index("cent")
    x = cent // 8
    yhi = (cent // 4) % 2
    z = cent % 4
    core = dp % 2
    ylo = dp // 2

    loads = [
        pltpu.make_async_copy(src, dst, in_sem.at[i])
        for i, (src, dst) in enumerate(((q_hbm, q_v), (c_hbm, c_v), (beta_hbm, beta_v), (ids_hbm, ids_v)))
    ]
    for load in loads:
        load.start()

    barrier = pltpu.get_barrier_semaphore()

    for r in range(1, 4):
        pl.semaphore_signal(barrier, inc=1, device_id=(dp, (((x + r) % 4) * 2 + yhi) * 4 + z), device_id_type=MESH)
        pl.semaphore_signal(barrier, inc=1, device_id=(dp, (x * 2 + yhi) * 4 + (z + r) % 4), device_id_type=MESH)
        pl.semaphore_signal(barrier, inc=1, device_id=((dp + r) % 4, cent), device_id_type=MESH)
    pl.semaphore_signal(barrier, inc=1, device_id=(dp, (x * 2 + 1 - yhi) * 4 + z), device_id_type=MESH)

    loads[0].wait()
    for i in range(4):
        block = pl.ds(i * (rows // 4), rows // 4)
        qf = q_v[block, :].astype(F32)
        inv = 1.0 / jnp.sqrt(jnp.sum(qf * qf, axis=1, keepdims=True) + EPS)
        qh_v[block, :] = (qf * inv).astype(BF16)

    loads[1].wait()
    loads[2].wait()
    loads[3].wait()
    tops = []
    for i in range(2):
        lanes = pl.ds(i * (rows // 2), rows // 2)
        cosine = dot(c_v[...], qh_v[lanes, :], NT)
        cos_v[:, lanes] = cosine
        score = cosine * beta_v[:, lanes]
        top = jnp.max(score, axis=0, keepdims=True)
        expo = jnp.exp(score - top)
        e_v[:, lanes] = expo
        lse_s[0, :, lanes] = top + jnp.log(jnp.sum(expo, axis=0, keepdims=True))
        tops.append(top)

    pl.semaphore_wait(barrier, 10)
    pl.semaphore_signal(ready_sem, inc=1, device_id=(dp, (x * 2 + 1 - yhi) * 4 + z), device_id_type=MESH)

    def line_copy(r):
        return pltpu.make_async_remote_copy(
            src_ref=lse_s.at[0], dst_ref=lse_r.at[r - 1], send_sem=lse_sem.at[0], recv_sem=lse_sem.at[1],
            device_id=(dp, (((x + r) % 4) * 2 + yhi) * 4 + z), device_id_type=MESH,
        )

    def plane_copy(r):
        return pltpu.make_async_remote_copy(
            src_ref=lse_s.at[1], dst_ref=lse_r.at[r + 2], send_sem=lse_sem.at[2], recv_sem=lse_sem.at[3],
            device_id=(dp, (x * 2 + (yhi + r // 4) % 2) * 4 + (z + r) % 4), device_id_type=MESH,
        )

    for r in (2, 1, 3):
        line_copy(r).start()

    qht_v[...] = qh_v[...].T
    ct_v[...] = c_v[...].T
    for i in range(2):
        lanes = pl.ds(i * (rows // 2), rows // 2)
        e = e_v[:, lanes]
        high = e.astype(BF16)
        low = (e - high.astype(F32)).astype(BF16)
        es_v[lanes, :] = dot(high, c_v[...], TN) + dot(low, c_v[...], TN)

    line = pl.ds(0, 3)
    pltpu.make_async_copy(lse_r.at[line], lse_r.at[line], lse_sem.at[1]).wait()
    lse_s[1] = join(lse_s[0], lse_r[0:3])
    for r in (1, 2, 3, 4):
        plane_copy(r).start()
    pl.semaphore_wait(ready_sem, 1)
    for r in (5, 6, 7):
        plane_copy(r).start()

    first = cent * cells
    for i in range(2):
        lanes = pl.ds(i * (rows // 2), rows // 2)
        cell_pos = lax.broadcasted_iota(jnp.int32, (cells, rows // 2), 0) + first
        count = jnp.zeros((cells, rows // 2), F32)
        for slot in range(slots):
            count = count + jnp.where(ids_v[slot : slot + 1, lanes] == cell_pos, SCALE / slots, 0.0)
        d_v[:, lanes] = count
        ts_v[lanes, :] = dot(count.astype(BF16), c_v[...], TN)

    plane = pl.ds(3, 7)
    pltpu.make_async_copy(lse_r.at[plane], lse_r.at[plane], lse_sem.at[3]).wait()
    lse = join(lse_s[1], lse_r[3:10])
    weight = jnp.exp(jnp.concatenate(tops, axis=1) - lse) * SCALE
    weight_col = jnp.broadcast_to(weight, (128, rows)).T

    for i in range(rows // 128):
        block = pl.ds(i * 128, 128)
        for j in range(3):
            cols = pl.ds(j * 128, 128)
            gx_s[i, :, cols] = (es_v[block, cols] * weight_col[i * 128 : (i + 1) * 128] - ts_v[block, cols]).astype(BF16)
        for j in range(3):
            cols = pl.ds(half + j * 128, 128)
            g = (es_v[block, cols] * weight_col[i * 128 : (i + 1) * 128] - ts_v[block, cols]).astype(BF16)
            for k in range(8):
                gz_s[k % 4, 2 * i + k // 4, :, pl.ds(j * 128, 128)] = g[k * 16 : (k + 1) * 16]

    def x_copy(to, r):
        return pltpu.make_async_remote_copy(
            src_ref=gx_s.at[to], dst_ref=gx_r.at[r - 1], send_sem=a_send.at[0, r - 1], recv_sem=a_recv.at[0, r - 1],
            device_id=(dp, (to * 2 + yhi) * 4 + z), device_id_type=MESH,
        )

    def z_copy(to, r):
        return pltpu.make_async_remote_copy(
            src_ref=gz_s.at[to], dst_ref=gz_r.at[r - 1], send_sem=a_send.at[1, r - 1], recv_sem=a_recv.at[1, r - 1],
            device_id=(dp, (x * 2 + yhi) * 4 + to), device_id_type=MESH,
        )

    for to in range(4):

        @pl.when(to != x)
        def _():
            x_copy(to, (to + 4 - x) % 4).start()

        @pl.when(to != z)
        def _():
            z_copy(to, (to + 4 - z) % 4).start()

    def grad_part(to, d):
        return dot(qht_v[pl.ds(pl.multiple_of(to * part, 64), part), :], d, NT)

    def core_copy(i):
        return pltpu.make_async_remote_copy(
            src_ref=core_s.at[i], dst_ref=core_r.at[i], send_sem=core_send.at[i], recv_sem=core_recv.at[i],
            device_id=(ylo * 2 + 1 - core, cent), device_id_type=MESH,
        )

    def y_copy(i):
        return pltpu.make_async_remote_copy(
            src_ref=y_s.at[i], dst_ref=y_r.at[i], send_sem=y_send.at[i], recv_sem=y_recv.at[i],
            device_id=((1 - ylo) * 2 + core, cent), device_id_type=MESH,
        )

    ds = []
    for i in range(2):
        block = pl.ds(i * (cells // 2), cells // 2)
        d = (e_v[block, :] * weight - d_v[block, :]).astype(BF16)
        ds.append(d)
        core_s[i] = grad_part((1 - ylo) * 2 + 1 - core, d).astype(BF16)
        core_copy(i).start()
    far = [grad_part((1 - ylo) * 2 + core, d) for d in ds]
    for i in range(2):
        core_copy(i).wait()
        y_s[i] = (far[i] + core_r[i].astype(F32)).astype(BF16)
        y_copy(i).start()
    for i in range(2):
        core_s[2 + i] = grad_part(ylo * 2 + 1 - core, ds[i]).astype(BF16)
        core_copy(2 + i).start()
    for i in range(2):
        near_v[i] = grad_part(dp, ds[i])

    for i in range(2):
        block = pl.ds(i * (cells // 2), cells // 2)
        prod = ds[i].astype(F32) * cos_v[block, :]
        prod = prod[:, 0:128] + prod[:, 128:256] + prod[:, 256:384] + prod[:, 384:512]
        row_s[:, block] = jnp.sum(prod.T, axis=0, keepdims=True)

    def row_copy(r):
        return pltpu.make_async_remote_copy(
            src_ref=row_s, dst_ref=row_r.at[r - 1], send_sem=row_sem.at[0, r - 1], recv_sem=row_sem.at[1, r - 1],
            device_id=((dp + r) % 4, cent), device_id_type=MESH,
        )

    for r in range(1, 4):
        row_copy(r).start()

    def bx_copy(to, r):
        return pltpu.make_async_remote_copy(
            src_ref=bx_s.at[to], dst_ref=bx_r.at[r - 1], send_sem=b_sem.at[0], recv_sem=b_sem.at[1],
            device_id=(dp, x * 8 + to), device_id_type=MESH,
        )

    def bz_copy(to, r):
        return pltpu.make_async_remote_copy(
            src_ref=bz_s.at[to], dst_ref=bz_r.at[r - 1], send_sem=b_sem.at[2], recv_sem=b_sem.at[3],
            device_id=(dp, to * 4 + z), device_id_type=MESH,
        )

    for r in range(1, 4):
        x_copy(0, r).wait()
    total = gx_s[x].astype(F32)
    for r in range(3):
        total = total + gx_r[r].astype(F32)
    bx_s[...] = total.astype(BF16).reshape(8, 16, half)

    @pl.loop(0, 8)
    def _(to):
        @pl.when(to != yhi * 4 + z)
        def _():
            bx_copy(to, ((to // 4 + 2 - yhi) % 2) * 4 + (to + 4 - z) % 4).start()

    for r in range(1, 4):
        z_copy(0, r).wait()
    total = gz_s[z].astype(F32)
    for r in range(3):
        total = total + gz_r[r].astype(F32)
    bz_s[...] = total.astype(BF16)

    @pl.loop(0, 8)
    def _(to):
        @pl.when(to != x * 2 + yhi)
        def _():
            bz_copy(to, ((to + 2 - yhi) % 2) * 4 + (to // 2 + 4 - x) % 4).start()

    for r in range(1, 4):
        row_copy(r).wait()
    rowdot = row_s[...] + row_r[0] + row_r[1] + row_r[2]
    own_rows = pl.ds(pl.multiple_of(dp * part, 64), part)
    for i in range(2):
        block = pl.ds(i * (cells // 2), cells // 2)
        core_copy(2 + i).wait()
        y_copy(i).wait()
        grad = near_v[i] + core_r[2 + i].astype(F32) + y_r[i].astype(F32)
        here = slice(i * (cells // 2), (i + 1) * (cells // 2))
        cg_ref[:, block] = grad - rowdot[:, here] * ct_v[own_rows, block].astype(F32)

    mine = pl.ds(pl.multiple_of(cent * 16, 16), 16)
    qf = q_v[mine, :].astype(F32)
    norm = jnp.sqrt(jnp.sum(qf * qf, axis=1, keepdims=True) + EPS)
    hat = qh_v[mine, :].astype(F32)
    pltpu.make_async_copy(bx_r, bx_r, b_sem.at[1]).wait()
    left = bx_s[yhi * 4 + z].astype(F32) + jnp.sum(bx_r[...].astype(F32), axis=0)
    pltpu.make_async_copy(bz_r, bz_r, b_sem.at[3]).wait()
    right = bz_s[x * 2 + yhi].astype(F32) + jnp.sum(bz_r[...].astype(F32), axis=0)
    grad = jnp.concatenate([left, right], axis=1)
    along = jnp.sum(grad * hat, axis=1, keepdims=True)
    qg_ref[...] = (grad - along * hat) / norm

    pltpu.make_async_copy(lse_r.at[line], lse_r.at[line], lse_sem.at[0]).wait()
    pltpu.make_async_copy(lse_r.at[plane], lse_r.at[plane], lse_sem.at[2]).wait()
    pltpu.make_async_copy(bx_r, bx_r, b_sem.at[0]).wait()
    pltpu.make_async_copy(bz_r, bz_r, b_sem.at[2]).wait()


def local(queries, centroids, beta, teacher_ids):
    rows, width = queries.shape
    cells = centroids.shape[0]
    slots = teacher_ids.shape[1]
    half, part = width // 2, width // 4
    dma = pltpu.SemaphoreType.DMA
    query_grad, centroid_grad = pl.pallas_call(
        kernel,
        out_shape=(
            jax.ShapeDtypeStruct((rows // 32, width), F32),
            jax.ShapeDtypeStruct((part, cells), F32),
        ),
        in_specs=[pl.BlockSpec(memory_space=pltpu.MemorySpace.HBM)] * 4,
        out_specs=[pl.BlockSpec(memory_space=pltpu.VMEM)] * 2,
        scratch_shapes=[
            pltpu.VMEM((rows, width), BF16),
            pltpu.VMEM((cells, width), BF16),
            pltpu.VMEM((1, rows), F32),
            pltpu.VMEM((slots, rows), jnp.int32),
            pltpu.VMEM((rows, width), BF16),
            pltpu.VMEM((width, rows), BF16),
            pltpu.VMEM((width, cells), BF16),
            pltpu.VMEM((cells, rows), F32),
            pltpu.VMEM((cells, rows), F32),
            pltpu.VMEM((cells, rows), F32),
            pltpu.VMEM((rows, width), F32),
            pltpu.VMEM((rows, width), F32),
            pltpu.VMEM((2, 1, rows), F32),
            pltpu.VMEM((10, 1, rows), F32),
            pltpu.VMEM((4, rows // 4, half), BF16),
            pltpu.VMEM((3, rows // 4, half), BF16),
            pltpu.VMEM((4, 8, 16, half), BF16),
            pltpu.VMEM((3, 8, 16, half), BF16),
            pltpu.VMEM((8, 16, half), BF16),
            pltpu.VMEM((7, 16, half), BF16),
            pltpu.VMEM((8, 16, half), BF16),
            pltpu.VMEM((7, 16, half), BF16),
            pltpu.VMEM((4, part, cells // 2), BF16),
            pltpu.VMEM((4, part, cells // 2), BF16),
            pltpu.VMEM((2, part, cells // 2), BF16),
            pltpu.VMEM((2, part, cells // 2), BF16),
            pltpu.VMEM((2, part, cells // 2), F32),
            pltpu.VMEM((1, cells), F32),
            pltpu.VMEM((3, 1, cells), F32),
            dma((4,)),
            dma((4,)),
            dma((2, 3)),
            dma((2, 3)),
            dma((4,)),
            dma((4,)),
            dma((4,)),
            dma((2,)),
            dma((2,)),
            dma((2, 3)),
            pltpu.SemaphoreType.REGULAR,
        ],
        compiler_params=pltpu.CompilerParams(
            collective_id=0, has_side_effects=True, vmem_limit_bytes=24 * 1024 * 1024
        ),
    )(queries, centroids, beta.reshape(1, rows), teacher_ids.T)
    return query_grad, centroid_grad.T


def solution(mesh):
    in_specs = (P("dp", None), P("cent", None), P("dp"), P("dp", None))
    out_specs = (P(("dp", "cent"), None), P("cent", "dp"))
    return jax.shard_map(local, mesh=mesh, in_specs=in_specs, out_specs=out_specs, check_vma=False)
```

time: 32.2 us -> 33.5 us (1.040)
  local copies, waits for them, and re-layouts: 2.61 us -> 5.07 us
  Pallas kernels: 28.7 us -> 27.5 us
    unnamed x3 -> x10, local copies, waits for them, and re-layouts: 0.62 us -> 5.07 us
    pallas_call x1 -> x0, local copies, waits for them, and re-layouts: 1.98 us -> none  [local(): pl.pallas_call(kernel, out_shape=(jax.ShapeDtypeStruct((rows // 32, width...]
    pallas_call x1, Pallas kernels: 28.7 us -> 27.5 us  [local(): pl.pallas_call(kernel, out_shape=(jax.ShapeDtypeStruct((rows // 32, width...]
where the time goes in v2:
time: 33.5 us; the launch traced here: 33.2 us
  Pallas kernels  27.5 us (82%)
  local copies, waits for them, and re-layouts  5.07 us (15%)
  between operations  0.65 us (2%)
    pallas_call x1, Pallas kernels, local(): pl.pallas_call(kernel, out_shape=(jax.ShapeDtypeStruct((rows // 32, width...  27.5 us
    unnamed x10, local copies, waits for them, and re-layouts  5.07 us

profile of v2, /device:TPU:1, one launch (start us, length us, event | category | flops | bytes accessed | tf_op | source)
XLA Modules:
  0.0 33.2 jit_solution(10592892503681306513)
XLA Ops:
  0.6 0.0 copy-start.3
  0.6 0.7 %copy-done.3 = f32[512]{0:T(512)S(1)} copy-done((f32[512]{0:T(512)S(1)}, f32[512]{0:T(512)}, u32[]{:S(2)}) %copy-start.3) | copy-done | bytes 2072
  1.3 0.0 copy-start
  1.3 1.1 %copy-done = bf16[512,768]{1,0:T(8,128)(2,1)S(1)} copy-done((bf16[512,768]{1,0:T(8,128)(2,1)S(1)}, bf16[512,768]{1,0:T(8,128)(2,1)}, u32[]{:S(2)}) %copy-start) | copy-done | bytes 786456
  2.4 0.0 copy-start.1
  2.4 1.1 %copy-done.1 = bf16[512,768]{1,0:T(8,128)(2,1)S(1)} copy-done((bf16[512,768]{1,0:T(8,128)(2,1)S(1)}, bf16[512,768]{1,0:T(8,128)(2,1)}, u32[]{:S(2)}) %copy-start.1) | copy-done | bytes 786456
  3.6 0.0 copy-start.2
  3.6 0.8 %copy-done.2 = s32[512,16]{0,1:T(8,128)S(1)} copy-done((s32[512,16]{0,1:T(8,128)S(1)}, s32[512,16]{0,1:T(8,128)}, u32[]{:S(2)}) %copy-start.2) | copy-done | bytes 32792
  4.3 27.5 %shard_map.59 = (f32[16,768]{1,0:T(8,128)S(1)}, f32[192,512]{1,0:T(8,128)S(1)}) custom-call(bf16[512,768]{1,0:T(8,128)(2,1)S(1)} %copy-done, bf16[512,768]{1,0:T(8,128)(2,1)S(1)} %copy-done.1, f32[1,512]{1,0:T(1,128)S(1)} %bitcast.5, s32[16,512]{1,0:T(8,128)S(1)} %bitcast.4), custom_call_target="tpu_custom_call" | custom-call | tf_op jit(solution)/shard_map/pallas_call | solution.py:298
  31.8 0.6 %copy.8 = f32[16,768]{1,0:T(8,128)} copy(f32[16,768]{1,0:T(8,128)S(1)} %get-tuple-element.8) | data formatting | bytes 98304
  32.4 0.7 %copy.9 = f32[512,192]{0,1:T(8,128)} copy(f32[512,192]{0,1:T(8,128)S(1)} %bitcast.3) | data formatting | bytes 786432
Async XLA Ops:
  0.6 0.7 %copy-start.3 = (f32[512]{0:T(512)S(1)}, f32[512]{0:T(512)}, u32[]{:S(2)}) copy-start(f32[512]{0:T(512)} %param.6) | copy-start | bytes 6148
  1.3 1.1 %copy-start = (bf16[512,768]{1,0:T(8,128)(2,1)S(1)}, bf16[512,768]{1,0:T(8,128)(2,1)}, u32[]{:S(2)}) copy-start(bf16[512,768]{1,0:T(8,128)(2,1)} %q_hbm.1) | copy-start | bytes 2359300
  2.4 1.1 %copy-start.1 = (bf16[512,768]{1,0:T(8,128)(2,1)S(1)}, bf16[512,768]{1,0:T(8,128)(2,1)}, u32[]{:S(2)}) copy-start(bf16[512,768]{1,0:T(8,128)(2,1)} %c_hbm.1) | copy-start | bytes 2359300
  3.6 0.8 %copy-start.2 = (s32[512,16]{0,1:T(8,128)S(1)}, s32[512,16]{0,1:T(8,128)}, u32[]{:S(2)}) copy-start(s32[512,16]{0,1:T(8,128)} %param.7) | copy-start | bytes 98308

commit v3 on v2

--- a/solution.py
+++ b/solution.py
@@ -289,13 +289,21 @@
     pltpu.make_async_copy(bz_r, bz_r, b_sem.at[2]).wait()
 
 
+def store_results(qg_v, cg_v, qg_hbm, cg_hbm, sem):
+    copies = [pltpu.make_async_copy(cg_v, cg_hbm, sem.at[0]), pltpu.make_async_copy(qg_v, qg_hbm, sem.at[1])]
+    for copy in copies:
+        copy.start()
+    for copy in copies:
+        copy.wait()
+
+
 def local(queries, centroids, beta, teacher_ids):
     rows, width = queries.shape
     cells = centroids.shape[0]
     slots = teacher_ids.shape[1]
     half, part = width // 2, width // 4
     dma = pltpu.SemaphoreType.DMA
-    query_grad, centroid_grad = pl.pallas_call(
+    results = pl.pallas_call(
         kernel,
         out_shape=(
             jax.ShapeDtypeStruct((rows // 32, width), F32),
@@ -348,7 +356,15 @@
         compiler_params=pltpu.CompilerParams(
             collective_id=0, has_side_effects=True, vmem_limit_bytes=24 * 1024 * 1024
         ),
-    )(queries, centroids, beta.reshape(1, rows), teacher_ids.T)
+    )(*[pltpu.with_memory_space_constraint(a, pltpu.MemorySpace.HBM) for a in (queries, centroids, beta.reshape(1, rows), teacher_ids.T)])
+    query_grad, centroid_grad = pl.pallas_call(
+        store_results,
+        out_shape=[jax.ShapeDtypeStruct(a.shape, a.dtype) for a in results],
+        in_specs=[pl.BlockSpec(memory_space=pltpu.VMEM)] * 2,
+        out_specs=[pl.BlockSpec(memory_space=pltpu.MemorySpace.HBM)] * 2,
+        scratch_shapes=[dma((2,))],
+        compiler_params=pltpu.CompilerParams(vmem_limit_bytes=1024 * 1024),
+    )(*results)
     return query_grad, centroid_grad.T
 
 

time: 33.5 us -> 29 us (0.87)
  local copies, waits for them, and re-layouts: 5.07 us -> 0 us
  Pallas kernels: 27.5 us -> 28.3 us
    unnamed x10 -> x0, local copies, waits for them, and re-layouts: 5.07 us -> none
    pallas_call x0 -> x1, Pallas kernels: none -> 0.77 us  [local(): pl.pallas_call(store_results, out_shape=[jax.ShapeDtypeStruct(a.shape, a....]
where the time goes in v3:
time: 29 us; the launch traced here: 28.9 us
  Pallas kernels  28.3 us (98%)
  between operations  0.64 us (2%)
    pallas_call x1, Pallas kernels, local(): pl.pallas_call(kernel, out_shape=(jax.ShapeDtypeStruct((rows // 32, width...  27.5 us
    pallas_call x1, Pallas kernels, local(): pl.pallas_call(store_results, out_shape=[jax.ShapeDtypeStruct(a.shape, a....  0.77 us

profile of v3, /device:TPU:1, one launch (start us, length us, event | category | flops | bytes accessed | tf_op | source)
XLA Modules:
  0.0 28.9 jit_solution(7221912832672993389)
XLA Ops:
  0.6 27.5 %shard_map.59 = (f32[16,768]{1,0:T(8,128)S(1)}, f32[192,512]{1,0:T(8,128)S(1)}) custom-call(bf16[512,768]{1,0:T(8,128)(2,1)} %q_hbm.1, bf16[512,768]{1,0:T(8,128)(2,1)} %c_hbm.1, f32[1,512]{1,0:T(1,128)} %bitcast.4, s32[16,512]{1,0:T(8,128)} %bitcast.3), custom_call_target="tpu_custom_call" | custom-call | tf_op jit(solution)/shard_map/pallas_call | solution.py:306
  28.1 0.8 %shard_map.60 = (f32[16,768]{1,0:T(8,128)}, f32[192,512]{1,0:T(8,128)}) custom-call(f32[16,768]{1,0:T(8,128)S(1)} %get-tuple-element.6.qg_v, f32[192,512]{1,0:T(8,128)S(1)} %get-tuple-element.7.cg_v), custom_call_target="tpu_custom_call" | custom-call | tf_op jit(solution)/shard_map/pallas_call | solution.py:360

commit v4 on v3

--- a/solution.py
+++ b/solution.py
@@ -30,9 +30,9 @@
     qg_ref, cg_ref,
     q_v, c_v, beta_v, ids_v,
     qh_v, qht_v, ct_v, cos_v, e_v, d_v,
-    es_v, ts_v,
-    lse_s, lse_r,
-    gx_s, gx_r, gz_s, gz_r,
+    w_v, lse_s, lse_r,
+    ex_s, ex_r, ez_s, ez_r,
+    tx_s, tx_r, tz_s, tz_r,
     bx_s, bx_r, bz_s, bz_r,
     core_s, core_r, y_s, y_r,
     near_v, row_s, row_r,
@@ -76,7 +76,6 @@
     loads[1].wait()
     loads[2].wait()
     loads[3].wait()
-    tops = []
     for i in range(2):
         lanes = pl.ds(i * (rows // 2), rows // 2)
         cosine = dot(c_v[...], qh_v[lanes, :], NT)
@@ -84,9 +83,9 @@
         score = cosine * beta_v[:, lanes]
         top = jnp.max(score, axis=0, keepdims=True)
         expo = jnp.exp(score - top)
-        e_v[:, lanes] = expo
-        lse_s[0, :, lanes] = top + jnp.log(jnp.sum(expo, axis=0, keepdims=True))
-        tops.append(top)
+        total = jnp.sum(expo, axis=0, keepdims=True)
+        lse_s[0, :, lanes] = top + jnp.log(total)
+        e_v[:, lanes] = expo * (1.0 / total)
 
     pl.semaphore_wait(barrier, 10)
     pl.semaphore_signal(ready_sem, inc=1, device_id=(dp, (x * 2 + 1 - yhi) * 4 + z), device_id_type=MESH)
@@ -103,17 +102,66 @@
             device_id=(dp, (x * 2 + (yhi + r // 4) % 2) * 4 + (z + r) % 4), device_id_type=MESH,
         )
 
+    def column_copy(r):
+        return pltpu.make_async_remote_copy(
+            src_ref=lse_s.at[0], dst_ref=lse_r.at[r + 9], send_sem=lse_sem.at[4], recv_sem=lse_sem.at[5],
+            device_id=(dp, (x * 2 + yhi) * 4 + (z + r) % 4), device_id_type=MESH,
+        )
+
     for r in (2, 1, 3):
         line_copy(r).start()
-
-    qht_v[...] = qh_v[...].T
-    ct_v[...] = c_v[...].T
+    for r in (2, 1, 3):
+        column_copy(r).start()
+
+    def x_copy(src, dst, kind, to, r):
+        return pltpu.make_async_remote_copy(
+            src_ref=src.at[to], dst_ref=dst.at[r - 1], send_sem=a_send.at[kind, r - 1], recv_sem=a_recv.at[kind, r - 1],
+            device_id=(dp, (to * 2 + yhi) * 4 + z), device_id_type=MESH,
+        )
+
+    def z_copy(src, dst, kind, to, r):
+        return pltpu.make_async_remote_copy(
+            src_ref=src.at[to], dst_ref=dst.at[r - 1], send_sem=a_send.at[kind, r - 1], recv_sem=a_recv.at[kind, r - 1],
+            device_id=(dp, (x * 2 + yhi) * 4 + to), device_id_type=MESH,
+        )
+
+    def send_blocks(targets, x_src, x_dst, z_src, z_dst, kind):
+        for to in targets:
+
+            @pl.when(to != x)
+            def _():
+                x_copy(x_src, x_dst, kind, to, (to + 4 - x) % 4).start()
+
+            @pl.when(to != z)
+            def _():
+                z_copy(z_src, z_dst, kind + 1, to, (to + 4 - z) % 4).start()
+
+    def put_blocks(i, g, x_src, z_src):
+        x_src[2 * i : 2 * i + 2] = g[:, :half].reshape(2, 128, half)
+        for k in range(16):
+            z_src[k % 4, 4 * i + k // 4] = g[k * 16 : (k + 1) * 16, half:]
+
     for i in range(2):
         lanes = pl.ds(i * (rows // 2), rows // 2)
-        e = e_v[:, lanes]
-        high = e.astype(BF16)
-        low = (e - high.astype(F32)).astype(BF16)
-        es_v[lanes, :] = dot(high, c_v[...], TN) + dot(low, c_v[...], TN)
+        put_blocks(i, dot(e_v[:, lanes].astype(BF16), c_v[...], TN).astype(BF16), ex_s, ez_s)
+    send_blocks((0, 1), ex_s, ex_r, ez_s, ez_r, 0)
+
+    ids = ids_v[...] - cent * cells
+    position = lax.broadcasted_iota(jnp.int32, (256, rows), 0).astype(F32).astype(BF16)
+    for h in range(cells // 256):
+        here = ids - h * 256
+        here = jnp.where((here >= 0) & (here < 256), here, -1).astype(F32)
+        count = jnp.zeros((256, rows), BF16)
+        for slot in range(slots):
+            hit = jnp.broadcast_to(here[slot : slot + 1], (256, rows)).astype(BF16) == position
+            count = count + jnp.where(hit, jnp.bfloat16(SCALE / slots), jnp.bfloat16(0.0))
+        d_v[pl.ds(h * 256, 256), :] = count
+    for i in range(2):
+        lanes = pl.ds(i * (rows // 2), rows // 2)
+        put_blocks(i, dot(d_v[:, lanes], c_v[...], TN).astype(BF16), tx_s, tz_s)
+    send_blocks((0, 1), tx_s, tx_r, tz_s, tz_r, 2)
+    send_blocks((2, 3), ex_s, ex_r, ez_s, ez_r, 0)
+    send_blocks((2, 3), tx_s, tx_r, tz_s, tz_r, 2)
 
     line = pl.ds(0, 3)
     pltpu.make_async_copy(lse_r.at[line], lse_r.at[line], lse_sem.at[1]).wait()
@@ -124,54 +172,15 @@
     for r in (5, 6, 7):
         plane_copy(r).start()
 
-    first = cent * cells
-    for i in range(2):
-        lanes = pl.ds(i * (rows // 2), rows // 2)
-        cell_pos = lax.broadcasted_iota(jnp.int32, (cells, rows // 2), 0) + first
-        count = jnp.zeros((cells, rows // 2), F32)
-        for slot in range(slots):
-            count = count + jnp.where(ids_v[slot : slot + 1, lanes] == cell_pos, SCALE / slots, 0.0)
-        d_v[:, lanes] = count
-        ts_v[lanes, :] = dot(count.astype(BF16), c_v[...], TN)
+    qht_v[...] = qh_v[...].T
+    ct_v[...] = c_v[...].T
 
     plane = pl.ds(3, 7)
     pltpu.make_async_copy(lse_r.at[plane], lse_r.at[plane], lse_sem.at[3]).wait()
     lse = join(lse_s[1], lse_r[3:10])
-    weight = jnp.exp(jnp.concatenate(tops, axis=1) - lse) * SCALE
-    weight_col = jnp.broadcast_to(weight, (128, rows)).T
-
-    for i in range(rows // 128):
-        block = pl.ds(i * 128, 128)
-        for j in range(3):
-            cols = pl.ds(j * 128, 128)
-            gx_s[i, :, cols] = (es_v[block, cols] * weight_col[i * 128 : (i + 1) * 128] - ts_v[block, cols]).astype(BF16)
-        for j in range(3):
-            cols = pl.ds(half + j * 128, 128)
-            g = (es_v[block, cols] * weight_col[i * 128 : (i + 1) * 128] - ts_v[block, cols]).astype(BF16)
-            for k in range(8):
-                gz_s[k % 4, 2 * i + k // 4, :, pl.ds(j * 128, 128)] = g[k * 16 : (k + 1) * 16]
-
-    def x_copy(to, r):
-        return pltpu.make_async_remote_copy(
-            src_ref=gx_s.at[to], dst_ref=gx_r.at[r - 1], send_sem=a_send.at[0, r - 1], recv_sem=a_recv.at[0, r - 1],
-            device_id=(dp, (to * 2 + yhi) * 4 + z), device_id_type=MESH,
-        )
-
-    def z_copy(to, r):
-        return pltpu.make_async_remote_copy(
-            src_ref=gz_s.at[to], dst_ref=gz_r.at[r - 1], send_sem=a_send.at[1, r - 1], recv_sem=a_recv.at[1, r - 1],
-            device_id=(dp, (x * 2 + yhi) * 4 + to), device_id_type=MESH,
-        )
-
-    for to in range(4):
-
-        @pl.when(to != x)
-        def _():
-            x_copy(to, (to + 4 - x) % 4).start()
-
-        @pl.when(to != z)
-        def _():
-            z_copy(to, (to + 4 - z) % 4).start()
+    column = pl.ds(10, 3)
+    pltpu.make_async_copy(lse_r.at[column], lse_r.at[column], lse_sem.at[5]).wait()
+    weight = jnp.exp(lse_s[0] - lse) * SCALE
 
     def grad_part(to, d):
         return dot(qht_v[pl.ds(pl.multiple_of(to * part, 64), part), :], d, NT)
@@ -191,36 +200,10 @@
     ds = []
     for i in range(2):
         block = pl.ds(i * (cells // 2), cells // 2)
-        d = (e_v[block, :] * weight - d_v[block, :]).astype(BF16)
+        d = (e_v[block, :] * weight - d_v[block, :].astype(F32)).astype(BF16)
         ds.append(d)
         core_s[i] = grad_part((1 - ylo) * 2 + 1 - core, d).astype(BF16)
         core_copy(i).start()
-    far = [grad_part((1 - ylo) * 2 + core, d) for d in ds]
-    for i in range(2):
-        core_copy(i).wait()
-        y_s[i] = (far[i] + core_r[i].astype(F32)).astype(BF16)
-        y_copy(i).start()
-    for i in range(2):
-        core_s[2 + i] = grad_part(ylo * 2 + 1 - core, ds[i]).astype(BF16)
-        core_copy(2 + i).start()
-    for i in range(2):
-        near_v[i] = grad_part(dp, ds[i])
-
-    for i in range(2):
-        block = pl.ds(i * (cells // 2), cells // 2)
-        prod = ds[i].astype(F32) * cos_v[block, :]
-        prod = prod[:, 0:128] + prod[:, 128:256] + prod[:, 256:384] + prod[:, 384:512]
-        row_s[:, block] = jnp.sum(prod.T, axis=0, keepdims=True)
-
-    def row_copy(r):
-        return pltpu.make_async_remote_copy(
-            src_ref=row_s, dst_ref=row_r.at[r - 1], send_sem=row_sem.at[0, r - 1], recv_sem=row_sem.at[1, r - 1],
-            device_id=((dp + r) % 4, cent), device_id_type=MESH,
-        )
-
-    for r in range(1, 4):
-        row_copy(r).start()
-
     def bx_copy(to, r):
         return pltpu.make_async_remote_copy(
             src_ref=bx_s.at[to], dst_ref=bx_r.at[r - 1], send_sem=b_sem.at[0], recv_sem=b_sem.at[1],
@@ -233,11 +216,15 @@
             device_id=(dp, to * 4 + z), device_id_type=MESH,
         )
 
-    for r in range(1, 4):
-        x_copy(0, r).wait()
-    total = gx_s[x].astype(F32)
+    weights = [weight] + [jnp.exp(lse_r[r] - lse) * SCALE for r in (0, 1, 2, 10, 11, 12)] + [weight]
+    w_v[...] = jnp.concatenate(weights, axis=0).T
+    for r in range(1, 4):
+        x_copy(ex_s, ex_r, 0, 0, r).wait()
+        x_copy(tx_s, tx_r, 2, 0, r).wait()
+    w = w_v[pl.ds(pl.multiple_of(x * 128, 128), 128), :]
+    total = ex_s[x].astype(F32) * w[:, 0:1] - tx_s[x].astype(F32)
     for r in range(3):
-        total = total + gx_r[r].astype(F32)
+        total = total + (ex_r[r].astype(F32) * w[:, r + 1 : r + 2] - tx_r[r].astype(F32))
     bx_s[...] = total.astype(BF16).reshape(8, 16, half)
 
     @pl.loop(0, 8)
@@ -247,17 +234,46 @@
             bx_copy(to, ((to // 4 + 2 - yhi) % 2) * 4 + (to + 4 - z) % 4).start()
 
     for r in range(1, 4):
-        z_copy(0, r).wait()
-    total = gz_s[z].astype(F32)
-    for r in range(3):
-        total = total + gz_r[r].astype(F32)
-    bz_s[...] = total.astype(BF16)
+        z_copy(ez_s, ez_r, 1, 0, r).wait()
+        z_copy(tz_s, tz_r, 3, 0, r).wait()
+    for g in range(8):
+        w = w_v[pl.ds(pl.multiple_of(g * 64 + z * 16, 16), 16), :]
+        total = ez_s[z, g].astype(F32) * w[:, 0:1] - tz_s[z, g].astype(F32)
+        for r in range(3):
+            total = total + (ez_r[r, g].astype(F32) * w[:, r + 4 : r + 5] - tz_r[r, g].astype(F32))
+        bz_s[g] = total.astype(BF16)
 
     @pl.loop(0, 8)
     def _(to):
         @pl.when(to != x * 2 + yhi)
         def _():
             bz_copy(to, ((to + 2 - yhi) % 2) * 4 + (to // 2 + 4 - x) % 4).start()
+
+    far = [grad_part((1 - ylo) * 2 + core, d) for d in ds]
+    for i in range(2):
+        core_copy(i).wait()
+        y_s[i] = (far[i] + core_r[i].astype(F32)).astype(BF16)
+        y_copy(i).start()
+    for i in range(2):
+        core_s[2 + i] = grad_part(ylo * 2 + 1 - core, ds[i]).astype(BF16)
+        core_copy(2 + i).start()
+    for i in range(2):
+        near_v[i] = grad_part(dp, ds[i])
+
+    for i in range(2):
+        block = pl.ds(i * (cells // 2), cells // 2)
+        prod = ds[i].astype(F32) * cos_v[block, :]
+        prod = prod[:, 0:128] + prod[:, 128:256] + prod[:, 256:384] + prod[:, 384:512]
+        row_s[:, block] = jnp.sum(prod.T, axis=0, keepdims=True)
+
+    def row_copy(r):
+        return pltpu.make_async_remote_copy(
+            src_ref=row_s, dst_ref=row_r.at[r - 1], send_sem=row_sem.at[0, r - 1], recv_sem=row_sem.at[1, r - 1],
+            device_id=((dp + r) % 4, cent), device_id_type=MESH,
+        )
+
+    for r in range(1, 4):
+        row_copy(r).start()
 
     for r in range(1, 4):
         row_copy(r).wait()
@@ -283,6 +299,7 @@
     along = jnp.sum(grad * hat, axis=1, keepdims=True)
     qg_ref[...] = (grad - along * hat) / norm
 
+    pltpu.make_async_copy(lse_r.at[column], lse_r.at[column], lse_sem.at[4]).wait()
     pltpu.make_async_copy(lse_r.at[line], lse_r.at[line], lse_sem.at[0]).wait()
     pltpu.make_async_copy(lse_r.at[plane], lse_r.at[plane], lse_sem.at[2]).wait()
     pltpu.make_async_copy(bx_r, bx_r, b_sem.at[0]).wait()
@@ -321,11 +338,14 @@
             pltpu.VMEM((width, cells), BF16),
             pltpu.VMEM((cells, rows), F32),
             pltpu.VMEM((cells, rows), F32),
-            pltpu.VMEM((cells, rows), F32),
-            pltpu.VMEM((rows, width), F32),
-            pltpu.VMEM((rows, width), F32),
+            pltpu.VMEM((cells, rows), BF16),
+            pltpu.VMEM((rows, 8), F32),
             pltpu.VMEM((2, 1, rows), F32),
-            pltpu.VMEM((10, 1, rows), F32),
+            pltpu.VMEM((13, 1, rows), F32),
+            pltpu.VMEM((4, rows // 4, half), BF16),
+            pltpu.VMEM((3, rows // 4, half), BF16),
+            pltpu.VMEM((4, 8, 16, half), BF16),
+            pltpu.VMEM((3, 8, 16, half), BF16),
             pltpu.VMEM((4, rows // 4, half), BF16),
             pltpu.VMEM((3, rows // 4, half), BF16),
             pltpu.VMEM((4, 8, 16, half), BF16),
@@ -342,9 +362,9 @@
             pltpu.VMEM((1, cells), F32),
             pltpu.VMEM((3, 1, cells), F32),
             dma((4,)),
-            dma((4,)),
-            dma((2, 3)),
-            dma((2, 3)),
+            dma((6,)),
+            dma((4, 3)),
+            dma((4, 3)),
             dma((4,)),
             dma((4,)),
             dma((4,)),

time: 29 us -> 30.2 us (1.041)
  Pallas kernels: 28.3 us -> 29.4 us
    pallas_call x1, Pallas kernels: 27.5 us -> 28.6 us  [local(): pl.pallas_call(kernel, out_shape=(jax.ShapeDtypeStruct((rows // 32, width...]
where the time goes in v4:
time: 30.2 us; the launch traced here: 30 us
  Pallas kernels  29.4 us (97%)
  between operations  0.64 us (2%)
    pallas_call x1, Pallas kernels, local(): pl.pallas_call(kernel, out_shape=(jax.ShapeDtypeStruct((rows // 32, width...  28.6 us
    pallas_call x1, Pallas kernels, local(): pl.pallas_call(store_results, out_shape=[jax.ShapeDtypeStruct(a.shape, a....  0.77 us

profile of v4, /device:TPU:1, one launch (start us, length us, event | category | flops | bytes accessed | tf_op | source)
XLA Modules:
  0.0 30.0 jit_solution(12409363029474651037)
XLA Ops:
  0.6 28.6 %shard_map.59 = (f32[16,768]{1,0:T(8,128)S(1)}, f32[192,512]{1,0:T(8,128)S(1)}) custom-call(bf16[512,768]{1,0:T(8,128)(2,1)} %q_hbm.1, bf16[512,768]{1,0:T(8,128)(2,1)} %c_hbm.1, f32[1,512]{1,0:T(1,128)} %bitcast.4, s32[16,512]{1,0:T(8,128)} %bitcast.3), custom_call_target="tpu_custom_call" | custom-call | tf_op jit(solution)/shard_map/pallas_call | solution.py:323
  29.3 0.8 %shard_map.60 = (f32[16,768]{1,0:T(8,128)}, f32[192,512]{1,0:T(8,128)}) custom-call(f32[16,768]{1,0:T(8,128)S(1)} %get-tuple-element.6.qg_v, f32[192,512]{1,0:T(8,128)S(1)} %get-tuple-element.7.cg_v), custom_call_target="tpu_custom_call" | custom-call | tf_op jit(solution)/shard_map/pallas_call | solution.py:380

commit v5 on v3

--- a/solution.py
+++ b/solution.py
@@ -31,7 +31,7 @@
     q_v, c_v, beta_v, ids_v,
     qh_v, qht_v, ct_v, cos_v, e_v, d_v,
     es_v, ts_v,
-    lse_s, lse_r,
+    lse_v, lse_s, lse_r, early_r,
     gx_s, gx_r, gz_s, gz_r,
     bx_s, bx_r, bz_s, bz_r,
     core_s, core_r, y_s, y_r,
@@ -66,6 +66,14 @@
         pl.semaphore_signal(barrier, inc=1, device_id=((dp + r) % 4, cent), device_id_type=MESH)
     pl.semaphore_signal(barrier, inc=1, device_id=(dp, (x * 2 + 1 - yhi) * 4 + z), device_id_type=MESH)
 
+    early = ((yhi == 0) & (x < 2)) & (z < 2)
+
+    @pl.when(early)
+    def _():
+        @pl.loop(1, 32)
+        def _(r):
+            pl.semaphore_signal(barrier, inc=1, device_id=(dp, (cent + r) % 32), device_id_type=MESH)
+
     loads[0].wait()
     for i in range(4):
         block = pl.ds(i * (rows // 4), rows // 4)
@@ -76,7 +84,6 @@
     loads[1].wait()
     loads[2].wait()
     loads[3].wait()
-    tops = []
     for i in range(2):
         lanes = pl.ds(i * (rows // 2), rows // 2)
         cosine = dot(c_v[...], qh_v[lanes, :], NT)
@@ -84,11 +91,18 @@
         score = cosine * beta_v[:, lanes]
         top = jnp.max(score, axis=0, keepdims=True)
         expo = jnp.exp(score - top)
-        e_v[:, lanes] = expo
-        lse_s[0, :, lanes] = top + jnp.log(jnp.sum(expo, axis=0, keepdims=True))
-        tops.append(top)
-
-    pl.semaphore_wait(barrier, 10)
+        total = jnp.sum(expo, axis=0, keepdims=True)
+        lse_s[0, :, lanes] = top + jnp.log(total)
+        e_v[:, lanes] = expo * (1.0 / total)
+
+    @pl.when(early)
+    def _():
+        pl.semaphore_wait(barrier, 13)
+
+    @pl.when(jnp.logical_not(early))
+    def _():
+        pl.semaphore_wait(barrier, 14)
+
     pl.semaphore_signal(ready_sem, inc=1, device_id=(dp, (x * 2 + 1 - yhi) * 4 + z), device_id_type=MESH)
 
     def line_copy(r):
@@ -103,17 +117,39 @@
             device_id=(dp, (x * 2 + (yhi + r // 4) % 2) * 4 + (z + r) % 4), device_id_type=MESH,
         )
 
+    def early_copy(to):
+        return pltpu.make_async_remote_copy(
+            src_ref=lse_s.at[0], dst_ref=early_r.at[(cent + 31 - to) % 32], send_sem=lse_sem.at[4], recv_sem=lse_sem.at[5],
+            device_id=(dp, to), device_id_type=MESH,
+        )
+
+    for to in (0, 1, 8, 9):
+
+        @pl.when(to != cent)
+        def _():
+            early_copy(to).start()
+
     for r in (2, 1, 3):
         line_copy(r).start()
 
+    for i in range(2):
+        lanes = pl.ds(i * (rows // 2), rows // 2)
+        es_v[lanes, :] = dot(e_v[:, lanes].astype(BF16), c_v[...], TN)
+    ids = ids_v[...] - cent * cells
+    position = lax.broadcasted_iota(jnp.int32, (256, rows), 0).astype(F32).astype(BF16)
+    for h in range(cells // 256):
+        here = ids - h * 256
+        here = jnp.where((here >= 0) & (here < 256), here, -1).astype(F32)
+        count = jnp.zeros((256, rows), BF16)
+        for slot in range(slots):
+            hit = jnp.broadcast_to(here[slot : slot + 1], (256, rows)).astype(BF16) == position
+            count = count + jnp.where(hit, jnp.bfloat16(SCALE / slots), jnp.bfloat16(0.0))
+        d_v[pl.ds(h * 256, 256), :] = count
+    for i in range(2):
+        lanes = pl.ds(i * (rows // 2), rows // 2)
+        ts_v[lanes, :] = dot(d_v[:, lanes], c_v[...], TN)
     qht_v[...] = qh_v[...].T
     ct_v[...] = c_v[...].T
-    for i in range(2):
-        lanes = pl.ds(i * (rows // 2), rows // 2)
-        e = e_v[:, lanes]
-        high = e.astype(BF16)
-        low = (e - high.astype(F32)).astype(BF16)
-        es_v[lanes, :] = dot(high, c_v[...], TN) + dot(low, c_v[...], TN)
 
     line = pl.ds(0, 3)
     pltpu.make_async_copy(lse_r.at[line], lse_r.at[line], lse_sem.at[1]).wait()
@@ -124,20 +160,19 @@
     for r in (5, 6, 7):
         plane_copy(r).start()
 
-    first = cent * cells
-    for i in range(2):
-        lanes = pl.ds(i * (rows // 2), rows // 2)
-        cell_pos = lax.broadcasted_iota(jnp.int32, (cells, rows // 2), 0) + first
-        count = jnp.zeros((cells, rows // 2), F32)
-        for slot in range(slots):
-            count = count + jnp.where(ids_v[slot : slot + 1, lanes] == cell_pos, SCALE / slots, 0.0)
-        d_v[:, lanes] = count
-        ts_v[lanes, :] = dot(count.astype(BF16), c_v[...], TN)
-
     plane = pl.ds(3, 7)
-    pltpu.make_async_copy(lse_r.at[plane], lse_r.at[plane], lse_sem.at[3]).wait()
-    lse = join(lse_s[1], lse_r[3:10])
-    weight = jnp.exp(jnp.concatenate(tops, axis=1) - lse) * SCALE
+
+    @pl.when(early)
+    def _():
+        pltpu.make_async_copy(early_r, early_r, lse_sem.at[5]).wait()
+        lse_v[...] = join(lse_s[0], early_r[...])
+
+    @pl.when(jnp.logical_not(early))
+    def _():
+        pltpu.make_async_copy(lse_r.at[plane], lse_r.at[plane], lse_sem.at[3]).wait()
+        lse_v[...] = join(lse_s[1], lse_r[3:10])
+
+    weight = jnp.exp(lse_s[0] - lse_v[...]) * SCALE
     weight_col = jnp.broadcast_to(weight, (128, rows)).T
 
     for i in range(rows // 128):
@@ -191,14 +226,15 @@
     ds = []
     for i in range(2):
         block = pl.ds(i * (cells // 2), cells // 2)
-        d = (e_v[block, :] * weight - d_v[block, :]).astype(BF16)
+        d = (e_v[block, :] * weight - d_v[block, :].astype(F32)).astype(BF16)
         ds.append(d)
         core_s[i] = grad_part((1 - ylo) * 2 + 1 - core, d).astype(BF16)
         core_copy(i).start()
-    far = [grad_part((1 - ylo) * 2 + core, d) for d in ds]
+    for i in range(2):
+        near_v[i] = grad_part((1 - ylo) * 2 + core, ds[i])
     for i in range(2):
         core_copy(i).wait()
-        y_s[i] = (far[i] + core_r[i].astype(F32)).astype(BF16)
+        y_s[i] = (near_v[i] + core_r[i].astype(F32)).astype(BF16)
         y_copy(i).start()
     for i in range(2):
         core_s[2 + i] = grad_part(ylo * 2 + 1 - core, ds[i]).astype(BF16)
@@ -285,6 +321,18 @@
 
     pltpu.make_async_copy(lse_r.at[line], lse_r.at[line], lse_sem.at[0]).wait()
     pltpu.make_async_copy(lse_r.at[plane], lse_r.at[plane], lse_sem.at[2]).wait()
+
+    @pl.when(early)
+    def _():
+        three = pl.ds(0, 3)
+        pltpu.make_async_copy(early_r.at[three], early_r.at[three], lse_sem.at[4]).wait()
+        pltpu.make_async_copy(lse_r.at[plane], lse_r.at[plane], lse_sem.at[3]).wait()
+
+    @pl.when(jnp.logical_not(early))
+    def _():
+        four = pl.ds(0, 4)
+        pltpu.make_async_copy(early_r.at[four], early_r.at[four], lse_sem.at[4]).wait()
+
     pltpu.make_async_copy(bx_r, bx_r, b_sem.at[0]).wait()
     pltpu.make_async_copy(bz_r, bz_r, b_sem.at[2]).wait()
 
@@ -321,11 +369,13 @@
             pltpu.VMEM((width, cells), BF16),
             pltpu.VMEM((cells, rows), F32),
             pltpu.VMEM((cells, rows), F32),
-            pltpu.VMEM((cells, rows), F32),
+            pltpu.VMEM((cells, rows), BF16),
             pltpu.VMEM((rows, width), F32),
             pltpu.VMEM((rows, width), F32),
+            pltpu.VMEM((1, rows), F32),
             pltpu.VMEM((2, 1, rows), F32),
             pltpu.VMEM((10, 1, rows), F32),
+            pltpu.VMEM((31, 1, rows), F32),
             pltpu.VMEM((4, rows // 4, half), BF16),
             pltpu.VMEM((3, rows // 4, half), BF16),
             pltpu.VMEM((4, 8, 16, half), BF16),
@@ -342,7 +392,7 @@
             pltpu.VMEM((1, cells), F32),
             pltpu.VMEM((3, 1, cells), F32),
             dma((4,)),
-            dma((4,)),
+            dma((6,)),
             dma((2, 3)),
             dma((2, 3)),
             dma((4,)),

time: 29 us -> 28.6 us (0.986)
  Pallas kernels: 28.3 us -> 27.8 us
    pallas_call x1, Pallas kernels: 27.5 us -> 27 us  [local(): pl.pallas_call(kernel, out_shape=(jax.ShapeDtypeStruct((rows // 32, width...]
where the time goes in v5:
time: 28.6 us; the launch traced here: 28.5 us
  Pallas kernels  27.8 us (97%)
  between operations  0.64 us (2%)
    pallas_call x1, Pallas kernels, local(): pl.pallas_call(kernel, out_shape=(jax.ShapeDtypeStruct((rows // 32, width...  27 us
    pallas_call x1, Pallas kernels, local(): pl.pallas_call(store_results, out_shape=[jax.ShapeDtypeStruct(a.shape, a....  0.77 us

profile of v5, /device:TPU:1, one launch (start us, length us, event | category | flops | bytes accessed | tf_op | source)
XLA Modules:
  0.0 28.5 jit_solution(14527263038517167628)
XLA Ops:
  0.6 27.0 %shard_map.59 = (f32[16,768]{1,0:T(8,128)S(1)}, f32[192,512]{1,0:T(8,128)S(1)}) custom-call(bf16[512,768]{1,0:T(8,128)(2,1)} %q_hbm.1, bf16[512,768]{1,0:T(8,128)(2,1)} %c_hbm.1, f32[1,512]{1,0:T(1,128)} %bitcast.4, s32[16,512]{1,0:T(8,128)} %bitcast.3), custom_call_target="tpu_custom_call" | custom-call | tf_op jit(solution)/shard_map/pallas_call | solution.py:354
  27.7 0.8 %shard_map.60 = (f32[16,768]{1,0:T(8,128)}, f32[192,512]{1,0:T(8,128)}) custom-call(f32[16,768]{1,0:T(8,128)S(1)} %get-tuple-element.6.qg_v, f32[192,512]{1,0:T(8,128)S(1)} %get-tuple-element.7.cg_v), custom_call_target="tpu_custom_call" | custom-call | tf_op jit(solution)/shard_map/pallas_call | solution.py:410

commit v6 on v5

--- a/solution.py
+++ b/solution.py
@@ -9,6 +9,7 @@
 
 EPS = 1e-06
 SCALE = 1024.0
+LOWEST = -1e30
 MESH = pl.DeviceIdType.MESH
 F32 = jnp.float32
 BF16 = jnp.bfloat16
@@ -20,9 +21,9 @@
     return lax.dot_general(a, b, dims, preferred_element_type=F32)
 
 
-def join(own, others):
-    top = jnp.maximum(jnp.max(others, axis=0), own)
-    return top + jnp.log(jnp.sum(jnp.exp(others - top[None]), axis=0) + jnp.exp(own - top))
+def join(parts):
+    top = jnp.max(parts, axis=0)
+    return top + jnp.log(jnp.sum(jnp.exp(parts - top[None]), axis=0))
 
 
 def kernel(
@@ -31,12 +32,12 @@
     q_v, c_v, beta_v, ids_v,
     qh_v, qht_v, ct_v, cos_v, e_v, d_v,
     es_v, ts_v,
-    lse_v, lse_s, lse_r, early_r,
+    lse_v, lse_s, stat_v, spare_v,
     gx_s, gx_r, gz_s, gz_r,
     bx_s, bx_r, bz_s, bz_r,
     core_s, core_r, y_s, y_r,
     near_v, row_s, row_r,
-    in_sem, lse_sem, a_send, a_recv, b_sem, core_send, core_recv, y_send, y_recv, row_sem, ready_sem,
+    in_sem, lse_send, lse_recv, a_send, a_recv, b_sem, core_send, core_recv, y_send, y_recv, row_sem, ready_sem,
 ):
     rows, width = q_hbm.shape
     cells = c_hbm.shape[0]
@@ -66,13 +67,23 @@
         pl.semaphore_signal(barrier, inc=1, device_id=((dp + r) % 4, cent), device_id_type=MESH)
     pl.semaphore_signal(barrier, inc=1, device_id=(dp, (x * 2 + 1 - yhi) * 4 + z), device_id_type=MESH)
 
-    early = ((yhi == 0) & (x < 2)) & (z < 2)
-
-    @pl.when(early)
-    def _():
-        @pl.loop(1, 32)
-        def _(r):
-            pl.semaphore_signal(barrier, inc=1, device_id=(dp, (cent + r) % 32), device_id_type=MESH)
+    def start_time(line_yhi, line_z):
+        return 27 * line_yhi + 11 * line_z + 2 * (line_z // 2)
+
+    now = start_time(yhi, z)
+    lines = [(i, start_time(i // 4, i % 4)) for i in range(8)]
+    own_line = yhi * 4 + z
+    earlier_lines = sum([jnp.where(time < now, 1, 0) for _, time in lines])
+    for i, time in lines:
+
+        @pl.when(time > now)
+        def _():
+            for to in range(4):
+                pl.semaphore_signal(barrier, inc=1, device_id=(dp, to * 8 + i), device_id_type=MESH)
+
+        @pl.when(time < now)
+        def _():
+            stat_v[i, 1:4] = jnp.full((3, 1, rows), LOWEST, F32)
 
     loads[0].wait()
     for i in range(4):
@@ -93,44 +104,38 @@
         expo = jnp.exp(score - top)
         total = jnp.sum(expo, axis=0, keepdims=True)
         lse_s[0, :, lanes] = top + jnp.log(total)
+        stat_v[own_line, x, :, lanes] = top + jnp.log(total)
         e_v[:, lanes] = expo * (1.0 / total)
 
-    @pl.when(early)
-    def _():
-        pl.semaphore_wait(barrier, 13)
-
-    @pl.when(jnp.logical_not(early))
-    def _():
-        pl.semaphore_wait(barrier, 14)
-
+    pl.semaphore_wait(barrier, 10 + 4 * earlier_lines)
     pl.semaphore_signal(ready_sem, inc=1, device_id=(dp, (x * 2 + 1 - yhi) * 4 + z), device_id_type=MESH)
 
     def line_copy(r):
         return pltpu.make_async_remote_copy(
-            src_ref=lse_s.at[0], dst_ref=lse_r.at[r - 1], send_sem=lse_sem.at[0], recv_sem=lse_sem.at[1],
-            device_id=(dp, (((x + r) % 4) * 2 + yhi) * 4 + z), device_id_type=MESH,
-        )
-
-    def plane_copy(r):
-        return pltpu.make_async_remote_copy(
-            src_ref=lse_s.at[1], dst_ref=lse_r.at[r + 2], send_sem=lse_sem.at[2], recv_sem=lse_sem.at[3],
-            device_id=(dp, (x * 2 + (yhi + r // 4) % 2) * 4 + (z + r) % 4), device_id_type=MESH,
-        )
-
-    def early_copy(to):
-        return pltpu.make_async_remote_copy(
-            src_ref=lse_s.at[0], dst_ref=early_r.at[(cent + 31 - to) % 32], send_sem=lse_sem.at[4], recv_sem=lse_sem.at[5],
-            device_id=(dp, to), device_id_type=MESH,
-        )
-
-    for to in (0, 1, 8, 9):
-
-        @pl.when(to != cent)
-        def _():
-            early_copy(to).start()
+            src_ref=lse_s.at[0], dst_ref=stat_v.at[own_line, x], send_sem=lse_send.at[8], recv_sem=lse_recv.at[8],
+            device_id=(dp, ((x + r) % 4) * 8 + own_line), device_id_type=MESH,
+        )
+
+    def early_copy(i, to):
+        return pltpu.make_async_remote_copy(
+            src_ref=lse_s.at[0], dst_ref=stat_v.at[own_line, x], send_sem=lse_send.at[i], recv_sem=lse_recv.at[own_line],
+            device_id=(dp, to * 8 + i), device_id_type=MESH,
+        )
+
+    def late_copy(i):
+        return pltpu.make_async_remote_copy(
+            src_ref=lse_s.at[1], dst_ref=stat_v.at[own_line, 0], send_sem=lse_send.at[i], recv_sem=lse_recv.at[own_line],
+            device_id=(dp, x * 8 + i), device_id_type=MESH,
+        )
 
     for r in (2, 1, 3):
         line_copy(r).start()
+    for i, time in lines:
+
+        @pl.when(time < now)
+        def _():
+            for to in range(4):
+                early_copy(i, to).start()
 
     for i in range(2):
         lanes = pl.ds(i * (rows // 2), rows // 2)
@@ -151,27 +156,27 @@
     qht_v[...] = qh_v[...].T
     ct_v[...] = c_v[...].T
 
-    line = pl.ds(0, 3)
-    pltpu.make_async_copy(lse_r.at[line], lse_r.at[line], lse_sem.at[1]).wait()
-    lse_s[1] = join(lse_s[0], lse_r[0:3])
-    for r in (1, 2, 3, 4):
-        plane_copy(r).start()
+    three = spare_v.at[pl.ds(0, 3)]
+    pltpu.make_async_copy(three, three, lse_recv.at[8]).wait()
+    lse_s[1] = join(stat_v[own_line])
     pl.semaphore_wait(ready_sem, 1)
-    for r in (5, 6, 7):
-        plane_copy(r).start()
-
-    plane = pl.ds(3, 7)
-
-    @pl.when(early)
-    def _():
-        pltpu.make_async_copy(early_r, early_r, lse_sem.at[5]).wait()
-        lse_v[...] = join(lse_s[0], early_r[...])
-
-    @pl.when(jnp.logical_not(early))
-    def _():
-        pltpu.make_async_copy(lse_r.at[plane], lse_r.at[plane], lse_sem.at[3]).wait()
-        lse_v[...] = join(lse_s[1], lse_r[3:10])
-
+    for i, time in lines:
+
+        @pl.when(time > now)
+        def _():
+            late_copy(i).start()
+
+    for i, time in lines:
+
+        @pl.when(time > now)
+        def _():
+            pltpu.make_async_copy(spare_v, spare_v, lse_recv.at[i]).wait()
+
+        @pl.when(time < now)
+        def _():
+            pltpu.make_async_copy(spare_v.at[0], spare_v.at[0], lse_recv.at[i]).wait()
+
+    lse_v[...] = join(stat_v[...].reshape(32, 1, rows))
     weight = jnp.exp(lse_s[0] - lse_v[...]) * SCALE
     weight_col = jnp.broadcast_to(weight, (128, rows)).T
 
@@ -319,19 +324,16 @@
     along = jnp.sum(grad * hat, axis=1, keepdims=True)
     qg_ref[...] = (grad - along * hat) / norm
 
-    pltpu.make_async_copy(lse_r.at[line], lse_r.at[line], lse_sem.at[0]).wait()
-    pltpu.make_async_copy(lse_r.at[plane], lse_r.at[plane], lse_sem.at[2]).wait()
-
-    @pl.when(early)
-    def _():
-        three = pl.ds(0, 3)
-        pltpu.make_async_copy(early_r.at[three], early_r.at[three], lse_sem.at[4]).wait()
-        pltpu.make_async_copy(lse_r.at[plane], lse_r.at[plane], lse_sem.at[3]).wait()
-
-    @pl.when(jnp.logical_not(early))
-    def _():
-        four = pl.ds(0, 4)
-        pltpu.make_async_copy(early_r.at[four], early_r.at[four], lse_sem.at[4]).wait()
+    pltpu.make_async_copy(three, three, lse_send.at[8]).wait()
+    for i, time in lines:
+
+        @pl.when(time < now)
+        def _():
+            pltpu.make_async_copy(spare_v, spare_v, lse_send.at[i]).wait()
+
+        @pl.when(time > now)
+        def _():
+            pltpu.make_async_copy(spare_v.at[0], spare_v.at[0], lse_send.at[i]).wait()
 
     pltpu.make_async_copy(bx_r, bx_r, b_sem.at[0]).wait()
     pltpu.make_async_copy(bz_r, bz_r, b_sem.at[2]).wait()
@@ -374,8 +376,8 @@
             pltpu.VMEM((rows, width), F32),
             pltpu.VMEM((1, rows), F32),
             pltpu.VMEM((2, 1, rows), F32),
-            pltpu.VMEM((10, 1, rows), F32),
-            pltpu.VMEM((31, 1, rows), F32),
+            pltpu.VMEM((8, 4, 1, rows), F32),
+            pltpu.VMEM((4, 1, rows), F32),
             pltpu.VMEM((4, rows // 4, half), BF16),
             pltpu.VMEM((3, rows // 4, half), BF16),
             pltpu.VMEM((4, 8, 16, half), BF16),
@@ -392,7 +394,8 @@
             pltpu.VMEM((1, cells), F32),
             pltpu.VMEM((3, 1, cells), F32),
             dma((4,)),
-            dma((6,)),
+            dma((9,)),
+            dma((9,)),
             dma((2, 3)),
             dma((2, 3)),
             dma((4,)),

time: 28.6 us -> 28.4 us (level)
  no operation moved by 1% of the time
where the time goes in v6:
time: 28.4 us; the launch traced here: 28.3 us
  Pallas kernels  27.7 us (98%)
  between operations  0.64 us (2%)
    pallas_call x1, Pallas kernels, local(): pl.pallas_call(kernel, out_shape=(jax.ShapeDtypeStruct((rows // 32, width...  26.9 us
    pallas_call x1, Pallas kernels, local(): pl.pallas_call(store_results, out_shape=[jax.ShapeDtypeStruct(a.shape, a....  0.77 us

profile of v6, /device:TPU:1, one launch (start us, length us, event | category | flops | bytes accessed | tf_op | source)
XLA Modules:
  0.0 28.3 jit_solution(13379653902964368442)
XLA Ops:
  0.6 26.9 %shard_map.59 = (f32[16,768]{1,0:T(8,128)S(1)}, f32[192,512]{1,0:T(8,128)S(1)}) custom-call(bf16[512,768]{1,0:T(8,128)(2,1)} %q_hbm.1, bf16[512,768]{1,0:T(8,128)(2,1)} %c_hbm.1, f32[1,512]{1,0:T(1,128)} %bitcast.4, s32[16,512]{1,0:T(8,128)} %bitcast.3), custom_call_target="tpu_custom_call" | custom-call | tf_op jit(solution)/shard_map/pallas_call | solution.py:356
  27.5 0.8 %shard_map.60 = (f32[16,768]{1,0:T(8,128)}, f32[192,512]{1,0:T(8,128)}) custom-call(f32[16,768]{1,0:T(8,128)S(1)} %get-tuple-element.6.qg_v, f32[192,512]{1,0:T(8,128)S(1)} %get-tuple-element.7.cg_v), custom_call_target="tpu_custom_call" | custom-call | tf_op jit(solution)/shard_map/pallas_call | solution.py:413

commit v7 on v6

--- a/solution.py
+++ b/solution.py
@@ -36,7 +36,7 @@
     gx_s, gx_r, gz_s, gz_r,
     bx_s, bx_r, bz_s, bz_r,
     core_s, core_r, y_s, y_r,
-    near_v, row_s, row_r,
+    near_v, far_v, diff_v, row_s, row_r,
     in_sem, lse_send, lse_recv, a_send, a_recv, b_sem, core_send, core_recv, y_send, y_recv, row_sem, ready_sem,
 ):
     rows, width = q_hbm.shape
@@ -159,10 +159,16 @@
     three = spare_v.at[pl.ds(0, 3)]
     pltpu.make_async_copy(three, three, lse_recv.at[8]).wait()
     lse_s[1] = join(stat_v[own_line])
+    for i, time in lines:
+
+        @pl.when((time > now) & ((i // 4 == yhi) | (i % 4 == z)))
+        def _():
+            late_copy(i).start()
+
     pl.semaphore_wait(ready_sem, 1)
     for i, time in lines:
 
-        @pl.when(time > now)
+        @pl.when((time > now) & (i // 4 != yhi) & (i % 4 != z))
         def _():
             late_copy(i).start()
 
@@ -184,34 +190,38 @@
         block = pl.ds(i * 128, 128)
         for j in range(3):
             cols = pl.ds(j * 128, 128)
-            gx_s[i, :, cols] = (es_v[block, cols] * weight_col[i * 128 : (i + 1) * 128] - ts_v[block, cols]).astype(BF16)
+            g = es_v[block, cols] * weight_col[i * 128 : (i + 1) * 128] - ts_v[block, cols]
+            gx_s[i, :, :, cols] = g.astype(BF16).reshape(8, 16, 128)
         for j in range(3):
             cols = pl.ds(half + j * 128, 128)
             g = (es_v[block, cols] * weight_col[i * 128 : (i + 1) * 128] - ts_v[block, cols]).astype(BF16)
             for k in range(8):
-                gz_s[k % 4, 2 * i + k // 4, :, pl.ds(j * 128, 128)] = g[k * 16 : (k + 1) * 16]
-
-    def x_copy(to, r):
-        return pltpu.make_async_remote_copy(
-            src_ref=gx_s.at[to], dst_ref=gx_r.at[r - 1], send_sem=a_send.at[0, r - 1], recv_sem=a_recv.at[0, r - 1],
+                gz_s[k % 4, 4 * (k // 4) + i, :, pl.ds(j * 128, 128)] = g[k * 16 : (k + 1) * 16]
+
+    def x_copy(p, to, r):
+        pair = pl.ds(2 * p, 2)
+        return pltpu.make_async_remote_copy(
+            src_ref=gx_s.at[to, pair], dst_ref=gx_r.at[r - 1, pair], send_sem=a_send.at[0, p, r - 1], recv_sem=a_recv.at[0, p, r - 1],
             device_id=(dp, (to * 2 + yhi) * 4 + z), device_id_type=MESH,
         )
 
-    def z_copy(to, r):
-        return pltpu.make_async_remote_copy(
-            src_ref=gz_s.at[to], dst_ref=gz_r.at[r - 1], send_sem=a_send.at[1, r - 1], recv_sem=a_recv.at[1, r - 1],
+    def z_copy(p, to, r):
+        pair = pl.ds(2 * p, 2)
+        return pltpu.make_async_remote_copy(
+            src_ref=gz_s.at[to, pair], dst_ref=gz_r.at[r - 1, pair], send_sem=a_send.at[1, p, r - 1], recv_sem=a_recv.at[1, p, r - 1],
             device_id=(dp, (x * 2 + yhi) * 4 + to), device_id_type=MESH,
         )
 
-    for to in range(4):
-
-        @pl.when(to != x)
-        def _():
-            x_copy(to, (to + 4 - x) % 4).start()
-
-        @pl.when(to != z)
-        def _():
-            z_copy(to, (to + 4 - z) % 4).start()
+    for p in range(4):
+        for to in range(4):
+
+            @pl.when(to != x)
+            def _():
+                x_copy(p, to, (to + 4 - x) % 4).start()
+
+            @pl.when(to != z)
+            def _():
+                z_copy(p, to, (to + 4 - z) % 4).start()
 
     def grad_part(to, d):
         return dot(qht_v[pl.ds(pl.multiple_of(to * part, 64), part), :], d, NT)
@@ -228,28 +238,39 @@
             device_id=((1 - ylo) * 2 + core, cent), device_id_type=MESH,
         )
 
-    ds = []
+    def centroid_start():
+        for i in range(2):
+            block = pl.ds(i * (cells // 2), cells // 2)
+            diff_v[block, :] = (e_v[block, :] * weight - d_v[block, :].astype(F32)).astype(BF16)
+            core_s[i] = grad_part((1 - ylo) * 2 + 1 - core, diff_v[block, :]).astype(BF16)
+            core_copy(i).start()
+        for i in range(2):
+            block = pl.ds(i * (cells // 2), cells // 2)
+            far_v[i] = grad_part((1 - ylo) * 2 + core, diff_v[block, :])
+
+    def centroid_cross():
+        for i in range(2):
+            core_copy(i).wait()
+            y_s[i] = (far_v[i] + core_r[i].astype(F32)).astype(BF16)
+            y_copy(i).start()
+
+    centroid_start()
+
+    @pl.when(yhi == 0)
+    def _():
+        centroid_cross()
+
     for i in range(2):
         block = pl.ds(i * (cells // 2), cells // 2)
-        d = (e_v[block, :] * weight - d_v[block, :].astype(F32)).astype(BF16)
-        ds.append(d)
-        core_s[i] = grad_part((1 - ylo) * 2 + 1 - core, d).astype(BF16)
-        core_copy(i).start()
-    for i in range(2):
-        near_v[i] = grad_part((1 - ylo) * 2 + core, ds[i])
-    for i in range(2):
-        core_copy(i).wait()
-        y_s[i] = (near_v[i] + core_r[i].astype(F32)).astype(BF16)
-        y_copy(i).start()
-    for i in range(2):
-        core_s[2 + i] = grad_part(ylo * 2 + 1 - core, ds[i]).astype(BF16)
+        core_s[2 + i] = grad_part(ylo * 2 + 1 - core, diff_v[block, :]).astype(BF16)
         core_copy(2 + i).start()
     for i in range(2):
-        near_v[i] = grad_part(dp, ds[i])
-
-    for i in range(2):
         block = pl.ds(i * (cells // 2), cells // 2)
-        prod = ds[i].astype(F32) * cos_v[block, :]
+        near_v[i] = grad_part(dp, diff_v[block, :])
+
+    for i in range(2):
+        block = pl.ds(i * (cells // 2), cells // 2)
+        prod = diff_v[block, :].astype(F32) * cos_v[block, :]
         prod = prod[:, 0:128] + prod[:, 128:256] + prod[:, 256:384] + prod[:, 384:512]
         row_s[:, block] = jnp.sum(prod.T, axis=0, keepdims=True)
 
@@ -271,34 +292,37 @@
     def bz_copy(to, r):
         return pltpu.make_async_remote_copy(
             src_ref=bz_s.at[to], dst_ref=bz_r.at[r - 1], send_sem=b_sem.at[2], recv_sem=b_sem.at[3],
-            device_id=(dp, to * 4 + z), device_id_type=MESH,
-        )
-
-    for r in range(1, 4):
-        x_copy(0, r).wait()
-    total = gx_s[x].astype(F32)
-    for r in range(3):
-        total = total + gx_r[r].astype(F32)
-    bx_s[...] = total.astype(BF16).reshape(8, 16, half)
-
-    @pl.loop(0, 8)
-    def _(to):
-        @pl.when(to != yhi * 4 + z)
-        def _():
-            bx_copy(to, ((to // 4 + 2 - yhi) % 2) * 4 + (to + 4 - z) % 4).start()
-
-    for r in range(1, 4):
-        z_copy(0, r).wait()
-    total = gz_s[z].astype(F32)
-    for r in range(3):
-        total = total + gz_r[r].astype(F32)
-    bz_s[...] = total.astype(BF16)
-
-    @pl.loop(0, 8)
-    def _(to):
-        @pl.when(to != x * 2 + yhi)
-        def _():
-            bz_copy(to, ((to + 2 - yhi) % 2) * 4 + (to // 2 + 4 - x) % 4).start()
+            device_id=(dp, (to % 4) * 8 + (to // 4) * 4 + z), device_id_type=MESH,
+        )
+
+    def pass_on(p):
+        pair = pl.ds(2 * p, 2)
+        for copy, own, mine, got, out, send in (
+            (x_copy, x, gx_s, gx_r, bx_s, bx_copy),
+            (z_copy, z, gz_s, gz_r, bz_s, bz_copy),
+        ):
+            for r in range(1, 4):
+                copy(p, 0, r).wait()
+            total = mine[own, pair].astype(F32)
+            for r in range(3):
+                total = total + got[r, pair].astype(F32)
+            out[pair] = total.astype(BF16)
+            place = z if send is bx_copy else x
+            for to in (2 * p, 2 * p + 1):
+
+                @pl.when(to != yhi * 4 + place)
+                def _():
+                    send(to, ((to // 4 + 2 - yhi) % 2) * 4 + (to % 4 + 4 - place) % 4).start()
+
+    pass_on(0)
+    pass_on(1)
+
+    @pl.when(yhi == 1)
+    def _():
+        centroid_cross()
+
+    pass_on(2)
+    pass_on(3)
 
     for r in range(1, 4):
         row_copy(r).wait()
@@ -319,7 +343,7 @@
     pltpu.make_async_copy(bx_r, bx_r, b_sem.at[1]).wait()
     left = bx_s[yhi * 4 + z].astype(F32) + jnp.sum(bx_r[...].astype(F32), axis=0)
     pltpu.make_async_copy(bz_r, bz_r, b_sem.at[3]).wait()
-    right = bz_s[x * 2 + yhi].astype(F32) + jnp.sum(bz_r[...].astype(F32), axis=0)
+    right = bz_s[yhi * 4 + x].astype(F32) + jnp.sum(bz_r[...].astype(F32), axis=0)
     grad = jnp.concatenate([left, right], axis=1)
     along = jnp.sum(grad * hat, axis=1, keepdims=True)
     qg_ref[...] = (grad - along * hat) / norm
@@ -378,8 +402,8 @@
             pltpu.VMEM((2, 1, rows), F32),
             pltpu.VMEM((8, 4, 1, rows), F32),
             pltpu.VMEM((4, 1, rows), F32),
-            pltpu.VMEM((4, rows // 4, half), BF16),
-            pltpu.VMEM((3, rows // 4, half), BF16),
+            pltpu.VMEM((4, 8, 16, half), BF16),
+            pltpu.VMEM((3, 8, 16, half), BF16),
             pltpu.VMEM((4, 8, 16, half), BF16),
             pltpu.VMEM((3, 8, 16, half), BF16),
             pltpu.VMEM((8, 16, half), BF16),
@@ -391,13 +415,15 @@
             pltpu.VMEM((2, part, cells // 2), BF16),
             pltpu.VMEM((2, part, cells // 2), BF16),
             pltpu.VMEM((2, part, cells // 2), F32),
+            pltpu.VMEM((2, part, cells // 2), F32),
+            pltpu.VMEM((cells, rows), BF16),
             pltpu.VMEM((1, cells), F32),
             pltpu.VMEM((3, 1, cells), F32),
             dma((4,)),
             dma((9,)),
             dma((9,)),
-            dma((2, 3)),
-            dma((2, 3)),
+            dma((2, 4, 3)),
+            dma((2, 4, 3)),
             dma((4,)),
             dma((4,)),
             dma((4,)),

time: 28.4 us -> 28.7 us (1.011)
  the two profiles are of different devices: /device:TPU:1 before, /device:TPU:24 now
where the time goes in v7:
time: 28.7 us; the launch traced here: 28.6 us
  Pallas kernels  27.9 us (97%)
  between operations  0.64 us (2%)
    pallas_call x1, Pallas kernels, local(): pl.pallas_call(kernel, out_shape=(jax.ShapeDtypeStruct((rows // 32, width...  27.1 us
    pallas_call x1, Pallas kernels, local(): pl.pallas_call(store_results, out_shape=[jax.ShapeDtypeStruct(a.shape, a....  0.77 us

profile of v7, /device:TPU:24, one launch (start us, length us, event | category | flops | bytes accessed | tf_op | source)
XLA Modules:
  0.0 28.6 jit_solution(5673299584416090784)
XLA Ops:
  0.6 27.1 %shard_map.59 = (f32[16,768]{1,0:T(8,128)S(1)}, f32[192,512]{1,0:T(8,128)S(1)}) custom-call(bf16[512,768]{1,0:T(8,128)(2,1)} %q_hbm.1, bf16[512,768]{1,0:T(8,128)(2,1)} %c_hbm.1, f32[1,512]{1,0:T(1,128)} %bitcast.4, s32[16,512]{1,0:T(8,128)} %bitcast.3), custom_call_target="tpu_custom_call" | custom-call | tf_op jit(solution)/shard_map/pallas_call | solution.py:380
  27.8 0.8 %shard_map.60 = (f32[16,768]{1,0:T(8,128)}, f32[192,512]{1,0:T(8,128)}) custom-call(f32[16,768]{1,0:T(8,128)S(1)} %get-tuple-element.6.qg_v, f32[192,512]{1,0:T(8,128)S(1)} %get-tuple-element.7.cg_v), custom_call_target="tpu_custom_call" | custom-call | tf_op jit(solution)/shard_map/pallas_call | solution.py:439

commit v8 on v7

--- a/solution.py
+++ b/solution.py
@@ -68,7 +68,7 @@
     pl.semaphore_signal(barrier, inc=1, device_id=(dp, (x * 2 + 1 - yhi) * 4 + z), device_id_type=MESH)
 
     def start_time(line_yhi, line_z):
-        return 27 * line_yhi + 11 * line_z + 2 * (line_z // 2)
+        return (27 - 17 * ylo) * line_yhi + 11 * line_z + 2 * (line_z // 2)
 
     now = start_time(yhi, z)
     lines = [(i, start_time(i // 4, i % 4)) for i in range(8)]
@@ -212,7 +212,7 @@
             device_id=(dp, (x * 2 + yhi) * 4 + to), device_id_type=MESH,
         )
 
-    for p in range(4):
+    for p in (0, 2, 1, 3):
         for to in range(4):
 
             @pl.when(to != x)
@@ -315,13 +315,13 @@
                     send(to, ((to // 4 + 2 - yhi) % 2) * 4 + (to % 4 + 4 - place) % 4).start()
 
     pass_on(0)
-    pass_on(1)
 
     @pl.when(yhi == 1)
     def _():
         centroid_cross()
 
     pass_on(2)
+    pass_on(1)
     pass_on(3)
 
     for r in range(1, 4):

time: 28.7 us -> 27.9 us (0.972)
  the two profiles are of different devices: /device:TPU:24 before, /device:TPU:16 now
where the time goes in v8:
time: 27.9 us; the launch traced here: 27.7 us
  Pallas kernels  27.1 us (97%)
  between operations  0.64 us (2%)
    pallas_call x1, Pallas kernels, local(): pl.pallas_call(kernel, out_shape=(jax.ShapeDtypeStruct((rows // 32, width...  26.3 us
    pallas_call x1, Pallas kernels, local(): pl.pallas_call(store_results, out_shape=[jax.ShapeDtypeStruct(a.shape, a....  0.77 us

profile of v8, /device:TPU:16, one launch (start us, length us, event | category | flops | bytes accessed | tf_op | source)
XLA Modules:
  0.0 27.7 jit_solution(17791295040195891935)
XLA Ops:
  0.6 26.3 %shard_map.59 = (f32[16,768]{1,0:T(8,128)S(1)}, f32[192,512]{1,0:T(8,128)S(1)}) custom-call(bf16[512,768]{1,0:T(8,128)(2,1)} %q_hbm.1, bf16[512,768]{1,0:T(8,128)(2,1)} %c_hbm.1, f32[1,512]{1,0:T(1,128)} %bitcast.4, s32[16,512]{1,0:T(8,128)} %bitcast.3), custom_call_target="tpu_custom_call" | custom-call | tf_op jit(solution)/shard_map/pallas_call | solution.py:380
  27.0 0.8 %shard_map.60 = (f32[16,768]{1,0:T(8,128)}, f32[192,512]{1,0:T(8,128)}) custom-call(f32[16,768]{1,0:T(8,128)S(1)} %get-tuple-element.6.qg_v, f32[192,512]{1,0:T(8,128)S(1)} %get-tuple-element.7.cg_v), custom_call_target="tpu_custom_call" | custom-call | tf_op jit(solution)/shard_map/pallas_call | solution.py:439

commit v9 on v5

--- a/solution.py
+++ b/solution.py
@@ -35,7 +35,7 @@
     gx_s, gx_r, gz_s, gz_r,
     bx_s, bx_r, bz_s, bz_r,
     core_s, core_r, y_s, y_r,
-    near_v, row_s, row_r,
+    near_v, far_v, diff_v, row_s, row_r,
     in_sem, lse_sem, a_send, a_recv, b_sem, core_send, core_recv, y_send, y_recv, row_sem, ready_sem,
 ):
     rows, width = q_hbm.shape
@@ -175,38 +175,43 @@
     weight = jnp.exp(lse_s[0] - lse_v[...]) * SCALE
     weight_col = jnp.broadcast_to(weight, (128, rows)).T
 
-    for i in range(rows // 128):
-        block = pl.ds(i * 128, 128)
-        for j in range(3):
-            cols = pl.ds(j * 128, 128)
-            gx_s[i, :, cols] = (es_v[block, cols] * weight_col[i * 128 : (i + 1) * 128] - ts_v[block, cols]).astype(BF16)
-        for j in range(3):
-            cols = pl.ds(half + j * 128, 128)
-            g = (es_v[block, cols] * weight_col[i * 128 : (i + 1) * 128] - ts_v[block, cols]).astype(BF16)
-            for k in range(8):
-                gz_s[k % 4, 2 * i + k // 4, :, pl.ds(j * 128, 128)] = g[k * 16 : (k + 1) * 16]
-
-    def x_copy(to, r):
-        return pltpu.make_async_remote_copy(
-            src_ref=gx_s.at[to], dst_ref=gx_r.at[r - 1], send_sem=a_send.at[0, r - 1], recv_sem=a_recv.at[0, r - 1],
+    def x_copy(p, to, r):
+        pair = pl.ds(2 * p, 2)
+        return pltpu.make_async_remote_copy(
+            src_ref=gx_s.at[to, pair], dst_ref=gx_r.at[r - 1, pair], send_sem=a_send.at[0], recv_sem=a_recv.at[0, p],
             device_id=(dp, (to * 2 + yhi) * 4 + z), device_id_type=MESH,
         )
 
-    def z_copy(to, r):
-        return pltpu.make_async_remote_copy(
-            src_ref=gz_s.at[to], dst_ref=gz_r.at[r - 1], send_sem=a_send.at[1, r - 1], recv_sem=a_recv.at[1, r - 1],
+    def z_copy(p, to, r):
+        pair = pl.ds(2 * p, 2)
+        return pltpu.make_async_remote_copy(
+            src_ref=gz_s.at[to, pair], dst_ref=gz_r.at[r - 1, pair], send_sem=a_send.at[1], recv_sem=a_recv.at[1, p],
             device_id=(dp, (x * 2 + yhi) * 4 + to), device_id_type=MESH,
         )
 
-    for to in range(4):
-
-        @pl.when(to != x)
-        def _():
-            x_copy(to, (to + 4 - x) % 4).start()
-
-        @pl.when(to != z)
-        def _():
-            z_copy(to, (to + 4 - z) % 4).start()
+    def weighted(first_row, count, first_col):
+        block = slice(first_row, first_row + count)
+        w = weight_col[block]
+        cols = [slice(first_col + 128 * j, first_col + 128 * (j + 1)) for j in range(3)]
+        return [(es_v[block, c] * w - ts_v[block, c]).astype(BF16) for c in cols]
+
+    for p in (0, 2, 1, 3):
+        for i in range(4):
+            for j, g in enumerate(weighted(i * 128 + 32 * p, 32, 0)):
+                gx_s[i, 2 * p : 2 * p + 2, :, 128 * j : 128 * (j + 1)] = g.reshape(2, 16, 128)
+        for i in (2 * (p % 2), 2 * (p % 2) + 1):
+            for j, g in enumerate(weighted(i * 128 + 64 * (p // 2), 64, half)):
+                for k in range(4):
+                    gz_s[k, 4 * (p // 2) + i, :, 128 * j : 128 * (j + 1)] = g[k * 16 : (k + 1) * 16]
+        for to in range(4):
+
+            @pl.when(to != x)
+            def _():
+                x_copy(p, to, (to + 4 - x) % 4).start()
+
+            @pl.when(to != z)
+            def _():
+                z_copy(p, to, (to + 4 - z) % 4).start()
 
     def grad_part(to, d):
         return dot(qht_v[pl.ds(pl.multiple_of(to * part, 64), part), :], d, NT)
@@ -223,34 +228,45 @@
             device_id=((1 - ylo) * 2 + core, cent), device_id_type=MESH,
         )
 
-    ds = []
+    def centroid_start():
+        for i in range(2):
+            block = pl.ds(i * (cells // 2), cells // 2)
+            diff_v[block, :] = (e_v[block, :] * weight - d_v[block, :].astype(F32)).astype(BF16)
+            core_s[i] = grad_part((1 - ylo) * 2 + 1 - core, diff_v[block, :]).astype(BF16)
+            core_copy(i).start()
+        for i in range(2):
+            block = pl.ds(i * (cells // 2), cells // 2)
+            far_v[i] = grad_part((1 - ylo) * 2 + core, diff_v[block, :])
+
+    def centroid_cross():
+        for i in range(2):
+            core_copy(i).wait()
+            y_s[i] = (far_v[i] + core_r[i].astype(F32)).astype(BF16)
+            y_copy(i).start()
+
+    centroid_start()
+
+    @pl.when(yhi == 0)
+    def _():
+        centroid_cross()
+
     for i in range(2):
         block = pl.ds(i * (cells // 2), cells // 2)
-        d = (e_v[block, :] * weight - d_v[block, :].astype(F32)).astype(BF16)
-        ds.append(d)
-        core_s[i] = grad_part((1 - ylo) * 2 + 1 - core, d).astype(BF16)
-        core_copy(i).start()
-    for i in range(2):
-        near_v[i] = grad_part((1 - ylo) * 2 + core, ds[i])
-    for i in range(2):
-        core_copy(i).wait()
-        y_s[i] = (near_v[i] + core_r[i].astype(F32)).astype(BF16)
-        y_copy(i).start()
-    for i in range(2):
-        core_s[2 + i] = grad_part(ylo * 2 + 1 - core, ds[i]).astype(BF16)
+        core_s[2 + i] = grad_part(ylo * 2 + 1 - core, diff_v[block, :]).astype(BF16)
         core_copy(2 + i).start()
     for i in range(2):
-        near_v[i] = grad_part(dp, ds[i])
-
-    for i in range(2):
         block = pl.ds(i * (cells // 2), cells // 2)
-        prod = ds[i].astype(F32) * cos_v[block, :]
+        near_v[i] = grad_part(dp, diff_v[block, :])
+
+    for i in range(2):
+        block = pl.ds(i * (cells // 2), cells // 2)
+        prod = diff_v[block, :].astype(F32) * cos_v[block, :]
         prod = prod[:, 0:128] + prod[:, 128:256] + prod[:, 256:384] + prod[:, 384:512]
         row_s[:, block] = jnp.sum(prod.T, axis=0, keepdims=True)
 
     def row_copy(r):
         return pltpu.make_async_remote_copy(
-            src_ref=row_s, dst_ref=row_r.at[r - 1], send_sem=row_sem.at[0, r - 1], recv_sem=row_sem.at[1, r - 1],
+            src_ref=row_s, dst_ref=row_r.at[r - 1], send_sem=row_sem.at[0], recv_sem=row_sem.at[1],
             device_id=((dp + r) % 4, cent), device_id_type=MESH,
         )
 
@@ -266,37 +282,39 @@
     def bz_copy(to, r):
         return pltpu.make_async_remote_copy(
             src_ref=bz_s.at[to], dst_ref=bz_r.at[r - 1], send_sem=b_sem.at[2], recv_sem=b_sem.at[3],
-            device_id=(dp, to * 4 + z), device_id_type=MESH,
-        )
-
-    for r in range(1, 4):
-        x_copy(0, r).wait()
-    total = gx_s[x].astype(F32)
-    for r in range(3):
-        total = total + gx_r[r].astype(F32)
-    bx_s[...] = total.astype(BF16).reshape(8, 16, half)
-
-    @pl.loop(0, 8)
-    def _(to):
-        @pl.when(to != yhi * 4 + z)
-        def _():
-            bx_copy(to, ((to // 4 + 2 - yhi) % 2) * 4 + (to + 4 - z) % 4).start()
-
-    for r in range(1, 4):
-        z_copy(0, r).wait()
-    total = gz_s[z].astype(F32)
-    for r in range(3):
-        total = total + gz_r[r].astype(F32)
-    bz_s[...] = total.astype(BF16)
-
-    @pl.loop(0, 8)
-    def _(to):
-        @pl.when(to != x * 2 + yhi)
-        def _():
-            bz_copy(to, ((to + 2 - yhi) % 2) * 4 + (to // 2 + 4 - x) % 4).start()
-
-    for r in range(1, 4):
-        row_copy(r).wait()
+            device_id=(dp, (to % 4) * 8 + (to // 4) * 4 + z), device_id_type=MESH,
+        )
+
+    def pass_on(p):
+        pair = pl.ds(2 * p, 2)
+        for axis, own, mine, got, out, send in (
+            (0, x, gx_s, gx_r, bx_s, bx_copy),
+            (1, z, gz_s, gz_r, bz_s, bz_copy),
+        ):
+            pltpu.make_async_copy(got.at[:, pair], got.at[:, pair], a_recv.at[axis, p]).wait()
+            total = mine[own, pair].astype(F32)
+            for r in range(3):
+                total = total + got[r, pair].astype(F32)
+            out[pair] = total.astype(BF16)
+            place = z if send is bx_copy else x
+            for to in (2 * p, 2 * p + 1):
+
+                @pl.when(to != yhi * 4 + place)
+                def _():
+                    send(to, ((to // 4 + 2 - yhi) % 2) * 4 + (to % 4 + 4 - place) % 4).start()
+
+    pass_on(0)
+
+    @pl.when(yhi == 1)
+    def _():
+        centroid_cross()
+
+    pass_on(2)
+    pass_on(1)
+    pass_on(3)
+
+    pltpu.make_async_copy(row_r, row_r, row_sem.at[0]).wait()
+    pltpu.make_async_copy(row_r, row_r, row_sem.at[1]).wait()
     rowdot = row_s[...] + row_r[0] + row_r[1] + row_r[2]
     own_rows = pl.ds(pl.multiple_of(dp * part, 64), part)
     for i in range(2):
@@ -314,7 +332,7 @@
     pltpu.make_async_copy(bx_r, bx_r, b_sem.at[1]).wait()
     left = bx_s[yhi * 4 + z].astype(F32) + jnp.sum(bx_r[...].astype(F32), axis=0)
     pltpu.make_async_copy(bz_r, bz_r, b_sem.at[3]).wait()
-    right = bz_s[x * 2 + yhi].astype(F32) + jnp.sum(bz_r[...].astype(F32), axis=0)
+    right = bz_s[yhi * 4 + x].astype(F32) + jnp.sum(bz_r[...].astype(F32), axis=0)
     grad = jnp.concatenate([left, right], axis=1)
     along = jnp.sum(grad * hat, axis=1, keepdims=True)
     qg_ref[...] = (grad - along * hat) / norm
@@ -333,6 +351,8 @@
         four = pl.ds(0, 4)
         pltpu.make_async_copy(early_r.at[four], early_r.at[four], lse_sem.at[4]).wait()
 
+    pltpu.make_async_copy(gx_r, gx_r, a_send.at[0]).wait()
+    pltpu.make_async_copy(gz_r, gz_r, a_send.at[1]).wait()
     pltpu.make_async_copy(bx_r, bx_r, b_sem.at[0]).wait()
     pltpu.make_async_copy(bz_r, bz_r, b_sem.at[2]).wait()
 
@@ -376,8 +396,8 @@
             pltpu.VMEM((2, 1, rows), F32),
             pltpu.VMEM((10, 1, rows), F32),
             pltpu.VMEM((31, 1, rows), F32),
-            pltpu.VMEM((4, rows // 4, half), BF16),
-            pltpu.VMEM((3, rows // 4, half), BF16),
+            pltpu.VMEM((4, 8, 16, half), BF16),
+            pltpu.VMEM((3, 8, 16, half), BF16),
             pltpu.VMEM((4, 8, 16, half), BF16),
             pltpu.VMEM((3, 8, 16, half), BF16),
             pltpu.VMEM((8, 16, half), BF16),
@@ -389,18 +409,20 @@
             pltpu.VMEM((2, part, cells // 2), BF16),
             pltpu.VMEM((2, part, cells // 2), BF16),
             pltpu.VMEM((2, part, cells // 2), F32),
+            pltpu.VMEM((2, part, cells // 2), F32),
+            pltpu.VMEM((cells, rows), BF16),
             pltpu.VMEM((1, cells), F32),
             pltpu.VMEM((3, 1, cells), F32),
             dma((4,)),
             dma((6,)),
-            dma((2, 3)),
-            dma((2, 3)),
+            dma((2,)),
+            dma((2, 4)),
             dma((4,)),
             dma((4,)),
             dma((4,)),
             dma((2,)),
             dma((2,)),
-            dma((2, 3)),
+            dma((2,)),
             pltpu.SemaphoreType.REGULAR,
         ],
         compiler_params=pltpu.CompilerParams(

time: 28.6 us -> 27.4 us (0.958)
  the two profiles are of different devices: /device:TPU:1 before, /device:TPU:16 now
where the time goes in v9:
time: 27.4 us; the launch traced here: 27.2 us
  Pallas kernels  26.6 us (97%)
  between operations  0.64 us (2%)
    pallas_call x1, Pallas kernels, local(): pl.pallas_call(kernel, out_shape=(jax.ShapeDtypeStruct((rows // 32, width...  25.8 us
    pallas_call x1, Pallas kernels, local(): pl.pallas_call(store_results, out_shape=[jax.ShapeDtypeStruct(a.shape, a....  0.77 us

profile of v9, /device:TPU:16, one launch (start us, length us, event | category | flops | bytes accessed | tf_op | source)
XLA Modules:
  0.0 27.2 jit_solution(5109950198472542008)
XLA Ops:
  0.6 25.8 %shard_map.59 = (f32[16,768]{1,0:T(8,128)S(1)}, f32[192,512]{1,0:T(8,128)S(1)}) custom-call(bf16[512,768]{1,0:T(8,128)(2,1)} %q_hbm.1, bf16[512,768]{1,0:T(8,128)(2,1)} %c_hbm.1, f32[1,512]{1,0:T(1,128)} %bitcast.4, s32[16,512]{1,0:T(8,128)} %bitcast.3), custom_call_target="tpu_custom_call" | custom-call | tf_op jit(solution)/shard_map/pallas_call | solution.py:374
  26.5 0.8 %shard_map.60 = (f32[16,768]{1,0:T(8,128)}, f32[192,512]{1,0:T(8,128)}) custom-call(f32[16,768]{1,0:T(8,128)S(1)} %get-tuple-element.6.qg_v, f32[192,512]{1,0:T(8,128)S(1)} %get-tuple-element.7.cg_v), custom_call_target="tpu_custom_call" | custom-call | tf_op jit(solution)/shard_map/pallas_call | solution.py:432

commit v10 on v9

--- a/solution.py
+++ b/solution.py
@@ -195,7 +195,7 @@
         cols = [slice(first_col + 128 * j, first_col + 128 * (j + 1)) for j in range(3)]
         return [(es_v[block, c] * w - ts_v[block, c]).astype(BF16) for c in cols]
 
-    for p in (0, 2, 1, 3):
+    def query_part(p):
         for i in range(4):
             for j, g in enumerate(weighted(i * 128 + 32 * p, 32, 0)):
                 gx_s[i, 2 * p : 2 * p + 2, :, 128 * j : 128 * (j + 1)] = g.reshape(2, 16, 128)
@@ -244,7 +244,11 @@
             y_s[i] = (far_v[i] + core_r[i].astype(F32)).astype(BF16)
             y_copy(i).start()
 
+    query_part(0)
     centroid_start()
+    query_part(2)
+    query_part(1)
+    query_part(3)
 
     @pl.when(yhi == 0)
     def _():

time: 27.4 us -> 27.1 us (0.989)
  Pallas kernels: 26.6 us -> 26.3 us
    pallas_call x1, Pallas kernels: 25.8 us -> 25.5 us  [local(): pl.pallas_call(kernel, out_shape=(jax.ShapeDtypeStruct((rows // 32, width...]
where the time goes in v10:
time: 27.1 us; the launch traced here: 26.9 us
  Pallas kernels  26.3 us (97%)
  between operations  0.64 us (2%)
    pallas_call x1, Pallas kernels, local(): pl.pallas_call(kernel, out_shape=(jax.ShapeDtypeStruct((rows // 32, width...  25.5 us
    pallas_call x1, Pallas kernels, local(): pl.pallas_call(store_results, out_shape=[jax.ShapeDtypeStruct(a.shape, a....  0.77 us

profile of v10, /device:TPU:16, one launch (start us, length us, event | category | flops | bytes accessed | tf_op | source)
XLA Modules:
  0.0 26.9 jit_solution(13919853889544158028)
XLA Ops:
  0.6 25.5 %shard_map.59 = (f32[16,768]{1,0:T(8,128)S(1)}, f32[192,512]{1,0:T(8,128)S(1)}) custom-call(bf16[512,768]{1,0:T(8,128)(2,1)} %q_hbm.1, bf16[512,768]{1,0:T(8,128)(2,1)} %c_hbm.1, f32[1,512]{1,0:T(1,128)} %bitcast.4, s32[16,512]{1,0:T(8,128)} %bitcast.3), custom_call_target="tpu_custom_call" | custom-call | tf_op jit(solution)/shard_map/pallas_call | solution.py:378
  26.2 0.8 %shard_map.60 = (f32[16,768]{1,0:T(8,128)}, f32[192,512]{1,0:T(8,128)}) custom-call(f32[16,768]{1,0:T(8,128)S(1)} %get-tuple-element.6.qg_v, f32[192,512]{1,0:T(8,128)S(1)} %get-tuple-element.7.cg_v), custom_call_target="tpu_custom_call" | custom-call | tf_op jit(solution)/shard_map/pallas_call | solution.py:436

commit v11 on v10

--- a/solution.py
+++ b/solution.py
@@ -148,9 +148,6 @@
     for i in range(2):
         lanes = pl.ds(i * (rows // 2), rows // 2)
         ts_v[lanes, :] = dot(d_v[:, lanes], c_v[...], TN)
-    qht_v[...] = qh_v[...].T
-    ct_v[...] = c_v[...].T
-
     line = pl.ds(0, 3)
     pltpu.make_async_copy(lse_r.at[line], lse_r.at[line], lse_sem.at[1]).wait()
     lse_s[1] = join(lse_s[0], lse_r[0:3])
@@ -160,6 +157,9 @@
     for r in (5, 6, 7):
         plane_copy(r).start()
 
+    qht_v[...] = qh_v[...].T
+    ct_v[...] = c_v[...].T
+
     plane = pl.ds(3, 7)
 
     @pl.when(early)
@@ -203,11 +203,16 @@
             for j, g in enumerate(weighted(i * 128 + 64 * (p // 2), 64, half)):
                 for k in range(4):
                     gz_s[k, 4 * (p // 2) + i, :, 128 * j : 128 * (j + 1)] = g[k * 16 : (k + 1) * 16]
+
+    def x_send(p):
         for to in range(4):
 
             @pl.when(to != x)
             def _():
                 x_copy(p, to, (to + 4 - x) % 4).start()
+
+    def z_send(p, targets):
+        for to in targets:
 
             @pl.when(to != z)
             def _():
@@ -245,10 +250,18 @@
             y_copy(i).start()
 
     query_part(0)
+    z_send(0, (0, 1))
+    x_send(0)
     centroid_start()
     query_part(2)
-    query_part(1)
-    query_part(3)
+    z_send(2, (0, 1))
+    x_send(2)
+    z_send(0, (2, 3))
+    z_send(2, (2, 3))
+    for p in (1, 3):
+        query_part(p)
+        x_send(p)
+        z_send(p, range(4))
 
     @pl.when(yhi == 0)
     def _():

time: 27.1 us -> 27.1 us (level)
  no operation moved by 1% of the time
where the time goes in v11:
time: 27.1 us; the launch traced here: 26.9 us
  Pallas kernels  26.3 us (97%)
  between operations  0.64 us (2%)
    pallas_call x1, Pallas kernels, local(): pl.pallas_call(kernel, out_shape=(jax.ShapeDtypeStruct((rows // 32, width...  25.5 us
    pallas_call x1, Pallas kernels, local(): pl.pallas_call(store_results, out_shape=[jax.ShapeDtypeStruct(a.shape, a....  0.77 us

profile of v11, /device:TPU:16, one launch (start us, length us, event | category | flops | bytes accessed | tf_op | source)
XLA Modules:
  0.0 26.9 jit_solution(6551705814303258826)
XLA Ops:
  0.6 25.5 %shard_map.59 = (f32[16,768]{1,0:T(8,128)S(1)}, f32[192,512]{1,0:T(8,128)S(1)}) custom-call(bf16[512,768]{1,0:T(8,128)(2,1)} %q_hbm.1, bf16[512,768]{1,0:T(8,128)(2,1)} %c_hbm.1, f32[1,512]{1,0:T(1,128)} %bitcast.4, s32[16,512]{1,0:T(8,128)} %bitcast.3), custom_call_target="tpu_custom_call" | custom-call | tf_op jit(solution)/shard_map/pallas_call | solution.py:391
  26.2 0.8 %shard_map.60 = (f32[16,768]{1,0:T(8,128)}, f32[192,512]{1,0:T(8,128)}) custom-call(f32[16,768]{1,0:T(8,128)S(1)} %get-tuple-element.6.qg_v, f32[192,512]{1,0:T(8,128)S(1)} %get-tuple-element.7.cg_v), custom_call_target="tpu_custom_call" | custom-call | tf_op jit(solution)/shard_map/pallas_call | solution.py:449

commit v12 on v11

--- a/solution.py
+++ b/solution.py
@@ -151,10 +151,10 @@
     line = pl.ds(0, 3)
     pltpu.make_async_copy(lse_r.at[line], lse_r.at[line], lse_sem.at[1]).wait()
     lse_s[1] = join(lse_s[0], lse_r[0:3])
-    for r in (1, 2, 3, 4):
+    for r in (4, 2, 3, 1):
         plane_copy(r).start()
     pl.semaphore_wait(ready_sem, 1)
-    for r in (5, 6, 7):
+    for r in (6, 5, 7):
         plane_copy(r).start()
 
     qht_v[...] = qh_v[...].T

time: 27.1 us -> 27 us (level)
  no operation moved by 1% of the time
where the time goes in v12:
time: 27 us; the launch traced here: 26.9 us
  Pallas kernels  26.3 us (97%)
  between operations  0.64 us (2%)
    pallas_call x1, Pallas kernels, local(): pl.pallas_call(kernel, out_shape=(jax.ShapeDtypeStruct((rows // 32, width...  25.5 us
    pallas_call x1, Pallas kernels, local(): pl.pallas_call(store_results, out_shape=[jax.ShapeDtypeStruct(a.shape, a....  0.77 us

profile of v12, /device:TPU:16, one launch (start us, length us, event | category | flops | bytes accessed | tf_op | source)
XLA Modules:
  0.0 26.9 jit_solution(1371845475694288161)
XLA Ops:
  0.6 25.5 %shard_map.59 = (f32[16,768]{1,0:T(8,128)S(1)}, f32[192,512]{1,0:T(8,128)S(1)}) custom-call(bf16[512,768]{1,0:T(8,128)(2,1)} %q_hbm.1, bf16[512,768]{1,0:T(8,128)(2,1)} %c_hbm.1, f32[1,512]{1,0:T(1,128)} %bitcast.4, s32[16,512]{1,0:T(8,128)} %bitcast.3), custom_call_target="tpu_custom_call" | custom-call | tf_op jit(solution)/shard_map/pallas_call | solution.py:391
  26.1 0.8 %shard_map.60 = (f32[16,768]{1,0:T(8,128)}, f32[192,512]{1,0:T(8,128)}) custom-call(f32[16,768]{1,0:T(8,128)S(1)} %get-tuple-element.6.qg_v, f32[192,512]{1,0:T(8,128)S(1)} %get-tuple-element.7.cg_v), custom_call_target="tpu_custom_call" | custom-call | tf_op jit(solution)/shard_map/pallas_call | solution.py:449
